TPU v7x, 256 devices: a whole 4x4x8 slice. The times are simulated.
256 devices in a mesh: dom: 64 (over z, x, core), grp: 4 (over y).
Axes of the slice: x: 4, y: 4, z: 8, core: 2. Of those that a mesh axis runs over, the one named last changes fastest.
Arguments:
- blocks: bfloat16 [12288, 6, 128, 128], P(('dom', 'grp')), may hold values from -0.21875 to 0.21875
- local_cols: int32 [12288, 4], P(('dom', 'grp')), may hold values from 0 to 191
- remote_refs: int32 [12288, 2], P(('dom', 'grp')), may hold values from 0 to 191
- send_blocks: int32 [64, 4, 64, 3], P('dom', 'grp'), may hold values from 0 to 47
- send_counts: int32 [64, 4, 64], P('dom', 'grp'), may hold values from 0 to 3
- probes: bfloat16 [64, 1572864], P(None, ('dom', 'grp')), may hold values from -6 to 6
Outputs:
- moments: float32 [3, 1572864], P(None, ('dom', 'grp'))
All inputs are finite; a program needn't handle non-finite values.
Results may differ from a plain program's by a relative error of at most 0.00064.
Values may be sent and summed in bfloat16 or wider, within the bound.
No kernel may reach another device: no remote copies, remote signals or barrier semaphores. Data moves between devices by JAX's collectives and lax.ppermute only.
A program may use at most 64 MiB of HBM per device.

v0:
```python
import functools
import math

import jax
import jax.numpy as jnp
from jax import lax
from jax.experimental import pallas as pl
from jax.experimental.pallas import tpu as pltpu
from jax.sharding import PartitionSpec as P


PROBES = 64
LOCAL = 4
REMOTE = 2
KMOM = 256
LANES = 4
STEP = 8
WIDE = 48
ZS, XS, CS = 8, 4, 2
PLANE = XS * CS
EARLY, LATE = (1, 7, 2, 6, 3), (5, 4)


def grant(mib):
    return pltpu.CompilerParams(vmem_limit_bytes=mib * 1024 * 1024)


HBM = pl.BlockSpec(memory_space=pltpu.HBM)
VMEM = pl.BlockSpec(memory_space=pltpu.VMEM)
ANY = pl.BlockSpec(memory_space=pl.ANY)
SMEM = pl.BlockSpec(memory_space=pltpu.SMEM)
DMA = pltpu.SemaphoreType.DMA


def jackson(order, total):
    angle = math.pi / (total + 1)
    return (
        (total - order + 1) * math.cos(order * angle) + math.sin(order * angle) / math.tan(angle)
    ) / (total + 1)


def pair_dot(fields, mats):
    left = jnp.concatenate(fields, axis=1)
    right = jnp.concatenate(mats, axis=1)
    return lax.dot_general(left, right, (((1,), (1,)), ((), ())), preferred_element_type=jnp.float32)


def start_wide(table_ref, count_ref, src_ref, send_ref, sem):
    rows = src_ref.shape[0] - 1
    peers, slots, part, _ = send_ref.shape
    probes = pl.ds(0, part)

    @pl.loop(0, peers, unroll=4)
    def _(d):
        count = count_ref[d]
        for s in range(slots):
            index = jnp.where(s < count, table_ref[s, 0, d], rows)
            pltpu.make_async_copy(src_ref.at[index, probes], send_ref.at[d, s], sem).start()


def start_slim(first, table_ref, count_ref, me_ref, src_ref, turn_refs, sem):
    rows = src_ref.shape[0] - 1
    part = turn_refs[0].shape[1]
    slots = turn_refs[0].shape[0] // ZS
    me = me_ref[0]
    probes = pl.ds(first, part)

    @pl.loop(0, ZS)
    def _(dz):
        z = (me // PLANE + dz) & (ZS - 1)
        for k, ref in enumerate(turn_refs):
            x = (me // CS + k // CS) & (XS - 1)
            core = (me + k) & (CS - 1)
            d = z * PLANE + x * CS + core
            for s in range(slots):
                index = jnp.where(s < count_ref[d], table_ref[s, 0, d], rows)
                pltpu.make_async_copy(src_ref.at[index, probes], ref.at[dz * slots + s], sem).start()


def wait_all(refs, sem):
    for ref in refs:
        pltpu.make_async_copy(ref, ref, sem).wait()


def load_fields(probes_ref, src_ref):
    rows, size = src_ref.shape[0] - 1, src_ref.shape[2]
    for r in range(rows):
        src_ref[r] = probes_ref[:, r * size:(r + 1) * size]
    src_ref[rows] = jnp.zeros_like(src_ref[rows])


def pack_wide_kernel(table_ref, count_ref, probes_ref, send_ref, src_ref, send_sem):
    load_fields(probes_ref, src_ref)
    start_wide(table_ref, count_ref, src_ref, send_ref, send_sem)
    wait_all([send_ref], send_sem)


def pack_wide(table, counts, probes, peers, slots, rows, size):
    kind = probes.dtype
    return pl.pallas_call(
        pack_wide_kernel,
        grid=(1,),
        in_specs=[SMEM, SMEM, pl.BlockSpec((WIDE, probes.shape[1]), lambda i: (0, 0))],
        out_specs=HBM,
        scratch_shapes=[pltpu.VMEM((rows + 1, WIDE, size), kind), DMA],
        out_shape=pltpu.HBM((peers, slots, WIDE, size), kind),
        compiler_params=grant(62),
        name="pack_wide",
    )(table, counts, probes)


def pack_slim_kernel(table_ref, count_ref, me_ref, probes_ref, own_ref, *rest):
    turn_refs, (src_ref, own_sem, turn_sem) = rest[:PLANE], rest[PLANE:]
    rows = own_ref.shape[0]
    load_fields(probes_ref, src_ref)
    own = pltpu.make_async_copy(src_ref.at[pl.ds(0, rows)], own_ref, own_sem)
    own.start()
    start_slim(WIDE, table_ref, count_ref, me_ref, src_ref, turn_refs, turn_sem)
    own.wait()
    wait_all(turn_refs, turn_sem)


def slim_shapes(peers, slots, slim, size, kind):
    return [pltpu.HBM((peers // PLANE * slots, slim, size), kind)] * PLANE


def pack_slim(table, counts, me, probes, peers, slots, rows, size):
    part, kind = probes.shape[0], probes.dtype
    return pl.pallas_call(
        pack_slim_kernel,
        in_specs=[SMEM, SMEM, SMEM, VMEM],
        out_specs=[HBM] * (1 + PLANE),
        scratch_shapes=[pltpu.VMEM((rows + 1, part, size), kind), DMA, DMA],
        out_shape=[pltpu.HBM((rows, part, size), kind)] + slim_shapes(peers, slots, part - WIDE, size, kind),
        compiler_params=grant(24),
        name="pack_slim",
    )(table, counts, me, probes)


def turn_kernel(*refs):
    got, out, (held_ref, in_sem, out_sem) = refs[:PLANE], refs[PLANE + 1:-3], refs[-3:]
    slots = out[0].shape[0] // PLANE
    for k, ref in enumerate(got):
        pltpu.make_async_copy(ref, held_ref.at[k], in_sem.at[k]).start()
    for k, ref in enumerate(got):
        pltpu.make_async_copy(ref, held_ref.at[k], in_sem.at[k]).wait()
        for dz, target in enumerate(out):
            pltpu.make_async_copy(
                held_ref.at[k, pl.ds(dz * slots, slots)], target.at[pl.ds(k * slots, slots)], out_sem
            ).start()
    wait_all(out, out_sem)


def turn(got, after):
    blocks, part, size = got[0].shape
    count = blocks // ZS * PLANE
    return pl.pallas_call(
        turn_kernel,
        in_specs=[ANY] * PLANE + [HBM],
        out_specs=[HBM] * ZS,
        scratch_shapes=[pltpu.VMEM((PLANE, blocks, part, size), got[0].dtype), DMA((PLANE,)), DMA],
        out_shape=[pltpu.HBM((count, part, size), got[0].dtype)] * ZS,
        compiler_params=grant(24),
        name="turn",
    )(*got, in_hbm(after))


def block_copy(blocks_ref, held_ref, sem, first, count, step):
    rows = pl.ds(step * STEP, STEP)
    return pltpu.make_async_copy(blocks_ref.at[rows, pl.ds(first, count)], held_ref.at[rows], sem.at[step])


def fetch_kernel(blocks_ref, close_ref, sem):
    copy = pltpu.make_async_copy(blocks_ref.at[:, pl.ds(0, LOCAL)], close_ref, sem)
    copy.start()
    copy.wait()


def fetch(blocks):
    rows, _, size, _ = blocks.shape
    return pl.pallas_call(
        fetch_kernel,
        in_specs=[HBM],
        out_specs=VMEM,
        scratch_shapes=[DMA],
        out_shape=pltpu.VMEM((rows, LOCAL, size, size), blocks.dtype),
        compiler_params=grant(24),
        name="fetch",
    )(in_hbm(blocks))


def local_products(lane_ref, pieces, blocks_ref, panel_ref, held_ref, panel_sem, sem, cols_ref, use, done=None):
    rows = pieces[0].shape[0]
    steps = rows // STEP
    me = lane_ref[0]
    copies = []
    for n, piece in enumerate(pieces):
        lane = lax.rem(me + LANES - n % LANES, LANES)
        probes = pl.ds(n // LANES * WIDE, piece.shape[1])
        copies.append(
            pltpu.make_async_copy(piece, panel_ref.at[pl.ds(lane * rows, rows), probes], panel_sem.at[n])
        )
    for copy in copies:
        copy.start()
    if blocks_ref is not None:
        for step in range(steps):
            block_copy(blocks_ref, held_ref, sem, 0, LOCAL, step).start()
    for copy in copies:
        copy.wait()

    @pl.loop(0, steps)
    def _(step):
        if blocks_ref is not None:
            block_copy(blocks_ref, held_ref, sem, 0, LOCAL, step).wait()
        for t in range(STEP):
            r = step * STEP + t
            total = None
            for j in range(0, LOCAL, 2):
                term = pair_dot(
                    [panel_ref[cols_ref[j + k, r]] for k in range(2)],
                    [held_ref[r, j + k] for k in range(2)],
                )
                total = term if total is None else total + term
            use(r, total)
        if done is not None:
            done(step)


def local_kernel(cols_ref, lane_ref, own_ref, prev_ref, across_ref, next_ref, close_ref, sum_ref, total_ref, total_sem, panel_ref, panel_sem):
    def use(r, total):
        total_ref[r] = total

    def done(step):
        at = pl.ds(step * STEP, STEP)
        pltpu.make_async_copy(total_ref.at[at], sum_ref.at[at], total_sem).start()

    pieces = (own_ref, prev_ref, across_ref, next_ref)
    local_products(lane_ref, pieces, None, panel_ref, close_ref, panel_sem, None, cols_ref, use, done)
    wait_all([sum_ref], total_sem)


def local_scratch(rows, part, size, kind):
    return [
        pltpu.VMEM((LANES * rows, part, size), kind),
        pltpu.VMEM((rows, LOCAL, size, size), kind),
        DMA((2 * LANES,)),
        DMA((rows // STEP,)),
    ]


def in_hbm(x):
    return pltpu.with_memory_space_constraint(x, pltpu.HBM)


def in_vmem(x):
    return pltpu.with_memory_space_constraint(x, pltpu.VMEM)


def local_part(cols, lane, pieces, close):
    rows, part, size = pieces[0].shape
    panel, _, panel_sem, _ = local_scratch(rows, part, size, close.dtype)
    return pl.pallas_call(
        local_kernel,
        in_specs=[SMEM, SMEM] + [ANY] * LANES + [VMEM],
        out_specs=HBM,
        scratch_shapes=[pltpu.VMEM((rows, part, size), jnp.float32), DMA, panel, panel_sem],
        out_shape=pltpu.HBM((rows, part, size), jnp.float32),
        compiler_params=grant(24),
        name="local",
    )(cols, lane, *pieces, in_vmem(close))


def row_copies(blocks_ref, other_ref, far_ref, near_ref, far_sem, near_sem, probes, step):
    at = pl.ds(step * STEP, STEP)
    near = pltpu.make_async_copy(other_ref.at[at, probes], near_ref.at[at], near_sem.at[step])
    return block_copy(blocks_ref, far_ref, far_sem, LOCAL, REMOTE, step), near


def remote_products(gather, left, blocks_ref, other_ref, probes, far_ref, near_ref, far_sem, near_sem, use):
    rows = near_ref.shape[0]
    steps = rows // STEP
    start, wait = gather
    for step in range(steps):
        start(step)
        for copy in row_copies(blocks_ref, other_ref, far_ref, near_ref, far_sem, near_sem, probes, step):
            copy.start()

    @pl.loop(0, steps)
    def _(step):
        wait(step)
        for copy in row_copies(blocks_ref, other_ref, far_ref, near_ref, far_sem, near_sem, probes, step):
            copy.wait()
        for t in range(STEP):
            r = step * STEP + t
            use(r, pair_dot([left(j, r) for j in range(REMOTE)], [far_ref[r, j] for j in range(REMOTE)]), near_ref[r])


def held_wide(refs_ref, got_ref):
    return (lambda step: None, lambda step: None), lambda j, r: got_ref[refs_ref[j, r]]


def gather_slim(refs_ref, got_refs, panel_ref, sem):
    copies = slim_copies(got_refs, panel_ref, sem)

    def start(step):
        if step == 0:
            for copy in copies:
                copy.start()

    def wait(step):
        @pl.when(step == 0)
        def _():
            for copy in copies:
                copy.wait()

    return (start, wait), lambda j, r: panel_ref[refs_ref[j, r]]


def remote_scratch(rows, part, size, kind, near_kind):
    return [
        pltpu.VMEM((rows, REMOTE, size, size), kind),
        pltpu.VMEM((rows, part, size), near_kind),
        DMA((rows // STEP,)),
        DMA((rows // STEP,)),
    ]


def slim_copies(got_refs, panel_ref, sem):
    count = got_refs[0].shape[0]
    return [
        pltpu.make_async_copy(ref, panel_ref.at[pl.ds(dz * count, count)], sem.at[dz]) for dz, ref in enumerate(got_refs)
    ]


def first_wide_kernel(refs_ref, table_ref, count_ref, got_ref, sum_ref, blocks_ref, own_ref, send_ref, src_ref, own_sem, send_sem, *scratch):
    rows, part, _ = own_ref.shape
    src_ref[rows] = jnp.zeros_like(src_ref[rows])

    def use(r, total, near):
        src_ref[r] = (near + total).astype(src_ref.dtype)

    gather, left = held_wide(refs_ref, got_ref)
    remote_products(gather, left, blocks_ref, sum_ref, pl.ds(0, part), *scratch, use)
    start_wide(table_ref, count_ref, src_ref, send_ref, send_sem)
    own = pltpu.make_async_copy(src_ref.at[pl.ds(0, rows)], own_ref, own_sem)
    own.start()
    own.wait()
    wait_all([send_ref], send_sem)


def first_wide(refs, table, counts, got, sums, blocks, peers, slots):
    rows, _, size = sums.shape
    kind = got.dtype
    return pl.pallas_call(
        first_wide_kernel,
        in_specs=[SMEM, SMEM, SMEM, VMEM, HBM, HBM],
        out_specs=[HBM, HBM],
        scratch_shapes=[pltpu.VMEM((rows + 1, WIDE, size), kind), DMA, DMA]
        + remote_scratch(rows, WIDE, size, kind, sums.dtype),
        out_shape=[pltpu.HBM((rows, WIDE, size), kind), pltpu.HBM((peers, slots, WIDE, size), kind)],
        compiler_params=grant(24),
        name="first_wide",
    )(in_hbm(refs), in_hbm(table), in_hbm(counts), in_vmem(got), in_hbm(sums), in_hbm(blocks))


def first_slim_kernel(refs_ref, table_ref, count_ref, me_ref, *rest):
    got_refs, (sum_ref, blocks_ref, own_ref), rest = rest[:ZS], rest[ZS:ZS + 3], rest[ZS + 3:]
    turn_refs, (src_ref, panel_ref, own_sem, turn_sem, got_sem), scratch = rest[:PLANE], rest[PLANE:PLANE + 5], rest[PLANE + 5:]
    rows, part, _ = own_ref.shape
    src_ref[rows] = jnp.zeros_like(src_ref[rows])

    def use(r, total, near):
        src_ref[r] = (near + total).astype(src_ref.dtype)

    gather, left = gather_slim(refs_ref, got_refs, panel_ref, got_sem)
    remote_products(gather, left, blocks_ref, sum_ref, pl.ds(WIDE, part), *scratch, use)
    start_slim(0, table_ref, count_ref, me_ref, src_ref, turn_refs, turn_sem)
    own = pltpu.make_async_copy(src_ref.at[pl.ds(0, rows)], own_ref, own_sem)
    own.start()
    own.wait()
    wait_all(turn_refs, turn_sem)


def first_slim(refs, table, counts, me, got, sums, blocks, peers, slots):
    rows, part, size = sums.shape
    slim, kind = part - WIDE, got[0].dtype
    return pl.pallas_call(
        first_slim_kernel,
        in_specs=[SMEM] * 4 + [ANY] * ZS + [HBM] * 2,
        out_specs=[HBM] * (1 + PLANE),
        scratch_shapes=[
            pltpu.VMEM((rows + 1, slim, size), kind),
            pltpu.VMEM((peers * slots, slim, size), kind),
            DMA,
            DMA,
            DMA((ZS,)),
        ]
        + remote_scratch(rows, slim, size, kind, sums.dtype),
        out_shape=[pltpu.HBM((rows, slim, size), kind)] + slim_shapes(peers, slots, slim, size, kind),
        compiler_params=grant(24),
        name="first_slim",
    )(refs, table, counts, me, *got, in_hbm(sums), in_hbm(blocks))


def near_kernel(scale, cols_ref, lane_ref, *rest):
    pieces, rest = rest[:2 * LANES], rest[2 * LANES:]
    blocks_ref, probes_ref, near_ref, base_ref, panel_ref, held_ref, base_sem, panel_sem, sem = rest
    rows, _, size = base_ref.shape
    copy = pltpu.make_async_copy(probes_ref, base_ref, base_sem)
    copy.start()
    copy.wait()
    me = lane_ref[0]

    def use(r, total):
        base = base_ref[r].astype(jnp.float32)
        one = panel_ref[me * rows + r].astype(jnp.float32)
        at = pl.ds(pl.multiple_of(r * size, size), size)
        for k, other in enumerate((base, one, 2.0 * total - base)):
            value = jnp.sum(base * other, axis=0, keepdims=True)
            near_ref[k:k + 1, at] = value if scale[k] is None else value * scale[k]

    local_products(lane_ref, pieces, blocks_ref, panel_ref, held_ref, panel_sem, sem, cols_ref, use)


def near_part(cols, lane, pieces, blocks, base, scale):
    rows, part, size = base.shape
    panel, held, panel_sem, sem = local_scratch(rows, part, size, blocks.dtype)
    return pl.pallas_call(
        functools.partial(near_kernel, scale),
        in_specs=[SMEM, SMEM] + [ANY] * (2 * LANES) + [HBM] * 2,
        out_specs=VMEM,
        scratch_shapes=[pltpu.VMEM(base.shape, base.dtype), panel, held, DMA, panel_sem, sem],
        out_shape=jax.ShapeDtypeStruct((3, rows * size), jnp.float32),
        compiler_params=grant(24),
        name="near",
    )(cols, lane, *pieces, in_hbm(blocks), in_hbm(base))


def moment_row(scale, near_ref, out_ref, size):
    out_ref[0:2] = near_ref[0:2]

    def use(r, total, base):
        at = pl.ds(pl.multiple_of(r * size, size), size)
        value = near_ref[2:3, at] + 2.0 * jnp.sum(total * base.astype(jnp.float32), axis=0, keepdims=True)
        out_ref[2:3, at] = value if scale is None else value * scale

    return use


def wide_kernel(refs_ref, wide_ref, near_ref, base_ref, blocks_ref, out_ref, far_ref, rest_ref, rest_sem, *scratch):
    rest = pltpu.make_async_copy(base_ref.at[:, pl.ds(WIDE, rest_ref.shape[1])], rest_ref, rest_sem)
    rest.start()
    use = moment_row(None, near_ref, out_ref, base_ref.shape[2])
    gather, left = held_wide(refs_ref, wide_ref)
    remote_products(gather, left, blocks_ref, base_ref, pl.ds(0, WIDE), far_ref, *scratch, use)
    rest.wait()


def wide_part(refs, wide, near, base, blocks):
    rows, part, size = base.shape
    far, *others = remote_scratch(rows, WIDE, size, blocks.dtype, base.dtype)
    return pl.pallas_call(
        wide_kernel,
        in_specs=[SMEM, VMEM, VMEM, HBM, HBM],
        out_specs=[VMEM] * 3,
        scratch_shapes=[DMA, *others],
        out_shape=[
            pltpu.VMEM(near.shape, near.dtype),
            pltpu.VMEM(far.shape, blocks.dtype),
            pltpu.VMEM((rows, part - WIDE, size), base.dtype),
        ],
        compiler_params=grant(24),
        name="wide",
    )(refs, in_vmem(wide), near, in_hbm(base), in_hbm(blocks))


def moments_kernel(scale, refs_ref, *rest):
    got_refs, (near_ref, far_ref, base_ref, out_ref, panel_ref, got_sem) = rest[:ZS], rest[ZS:]
    copies = slim_copies(got_refs, panel_ref, got_sem)
    for copy in copies:
        copy.start()
    rows, _, size = base_ref.shape
    use = moment_row(scale, near_ref, out_ref, size)
    for copy in copies:
        copy.wait()

    @pl.loop(0, rows // STEP)
    def _(step):
        for t in range(STEP):
            r = step * STEP + t
            left = [panel_ref[refs_ref[j, r]] for j in range(REMOTE)]
            use(r, pair_dot(left, [far_ref[r, j] for j in range(REMOTE)]), base_ref[r])


def moments_part(refs, got, near, far, base, scale):
    _, slim, size = base.shape
    return pl.pallas_call(
        functools.partial(moments_kernel, scale),
        in_specs=[SMEM] + [ANY] * ZS + [VMEM] * 3,
        out_specs=VMEM,
        scratch_shapes=[pltpu.VMEM((ZS * got[0].shape[0], slim, size), base.dtype), DMA((ZS,))],
        out_shape=jax.ShapeDtypeStruct(near.shape, near.dtype),
        compiler_params=grant(24),
        name="moments",
    )(refs, *got, in_vmem(near), in_vmem(far), in_vmem(base))


def plane_step(i, k):
    z, x, core = i // PLANE, i // CS % XS, i % CS
    return z * PLANE + (x + k // CS) % XS * CS + (core + k) % CS


def across_plane(sends):
    size = ZS * PLANE
    return [sends[0]] + [
        lax.ppermute(sends[k], "dom", [(i, plane_step(i, k)) for i in range(size)]) for k in range(1, PLANE)
    ]


def along_z(sends, steps):
    size = ZS * PLANE
    return {dz: lax.ppermute(sends[dz], "dom", [(i, (i + dz * PLANE) % size) for i in range(size)]) for dz in steps}


def slim_kernel(me_ref, refs_ref, out_ref, *, slots):
    me = me_ref[0]
    refs = refs_ref[...]
    e = refs // slots
    dz = (me // PLANE - e // PLANE) & (ZS - 1)
    dx = (me // CS - e // CS) & (XS - 1)
    core = (me - e) & (CS - 1)
    out_ref[...] = (dz * PLANE + dx * CS + core) * slots + refs - e * slots


def slim_slots(refs, slots, me):
    return pl.pallas_call(
        functools.partial(slim_kernel, slots=slots),
        in_specs=[SMEM, VMEM],
        out_specs=VMEM,
        out_shape=jax.ShapeDtypeStruct(refs.shape, refs.dtype),
        compiler_params=grant(24),
        name="slim_slots",
    )(me, refs)


def on_device(blocks, local_cols, remote_refs, send_blocks, send_counts, probes):
    rows, _, size, _ = blocks.shape
    peers, slots = send_blocks.shape[2], send_blocks.shape[3]
    table = send_blocks.transpose(0, 3, 1, 2)[0]
    counts = send_counts[0, 0]
    cols = local_cols.T
    refs = remote_refs.T
    lane = lax.axis_index("grp").astype(jnp.int32).reshape(1)
    me = lax.axis_index("dom").astype(jnp.int32).reshape(1)
    norm = 1.0 / math.sqrt(PROBES)
    scale = (
        jackson(0, KMOM) * norm,
        2.0 * jackson(1, KMOM) * norm,
        2.0 * jackson(2, KMOM) * norm,
    )

    def exchange(send):
        got = lax.all_to_all(send, "dom", split_axis=0, concat_axis=0, tiled=True)
        return got.reshape(peers * slots, send.shape[2], size)

    def panel(own):
        pieces = [own]
        for shift in (1, 2, 3):
            pieces.append(lax.ppermute(own, "grp", [(i, (i + shift) % LANES) for i in range(LANES)]))
        return pieces

    send = pack_wide(table, counts, probes, peers, slots, rows, size)
    wide = exchange(send)
    base, *sides = pack_slim(table, counts, me, probes, peers, slots, rows, size)
    sides = across_plane(sides)
    pieces = panel(base)
    sides = turn(sides, base)
    slim = {0: sides[0]} | along_z(sides, EARLY)
    close = fetch(blocks)
    sums = local_part(cols, lane, pieces, close)
    slim |= along_z(sides, LATE)
    slim = [slim[dz] for dz in range(ZS)]
    slim_refs = slim_slots(refs, slots, me)
    first, send = first_wide(refs, table, counts, wide, sums, blocks, peers, slots)
    wide = exchange(send)
    pieces = panel(first)
    slim_first, *sides = first_slim(slim_refs, table, counts, me, slim, sums, blocks, peers, slots)
    sides = across_plane(sides)
    pieces = pieces + panel(slim_first)
    sides = turn(sides, slim_first)
    slim = {0: sides[0]} | along_z(sides, (4, 3, 5, 2, 6, 1, 7))
    slim = [slim[dz] for dz in range(ZS)]
    near = near_part(cols, lane, pieces, blocks, base, scale[:2] + (None,))
    near, far, rest = wide_part(refs, wide, near, base, blocks)
    return moments_part(slim_refs, slim, near, far, rest, scale[2])


def solution(mesh):
    in_specs = (
        P(("dom", "grp"), None, None, None),
        P(("dom", "grp"), None),
        P(("dom", "grp"), None),
        P("dom", "grp", None, None),
        P("dom", "grp", None),
        P(None, ("dom", "grp")),
    )
    out_specs = P(None, ("dom", "grp"))

    return jax.shard_map(on_device, mesh=mesh, in_specs=in_specs, out_specs=out_specs, check_vma=False)
```

profile of v0, /device:TPU:16, one launch (start us, length us, event | category | flops | bytes accessed | tf_op | source)
XLA Modules:
  0.0 247.3 jit_solution(685285418974193615)
XLA Ops:
  0.0 2.7 %pack_wide.1 = bf16[64,3,48,128]{3,2,1,0:T(8,128)(2,1)} custom-call(s32[3,1,64]{2,1,0:T(1,128)} %bitcast.12, s32[64]{0:T(128)} %bitcast.21, bf16[64,6144]{1,0:T(8,128)(2,1)} %probes_ref.3), custom_call_target="tpu_custom_call" | custom-call | tf_op jit(solution)/shard_map/pack_wide/pallas_call | solution.py:100
  2.7 12.1 %all-to-all-start = ((bf16[64,3,48,128]{3,2,1,0:T(8,128)(2,1)}), bf16[64,3,48,128]{3,2,1,0:T(8,128)(2,1)S(1)}, u32[]{:S(2)}, u32[]{:S(2)}) async-start(bf16[64,3,48,128]{3,2,1,0:T(8,128)(2,1)} %pack_wide.1), calls=%async_computation | async-start | bytes 4718592 | tf_op jit(solution)/shard_map/all_to_all | solution.py:563
  14.8 2.3 pack_slim.1
  20.2 2.9 %fetch.1.close_ref = bf16[48,4,128,128]{3,2,1,0:T(8,128)(2,1)S(1)} custom-call(bf16[48,6,128,128]{3,2,1,0:T(8,128)(2,1)} %blocks_ref.5), custom_call_target="tpu_custom_call" | custom-call | tf_op jit(solution)/shard_map/fetch/pallas_call | solution.py:181
  23.0 30.8 %collective-permute-done.14.prev_ref = bf16[48,64,128]{2,1,0:T(8,128)(2,1)} collective-permute-done((bf16[48,64,128]{2,1,0:T(8,128)(2,1)}, bf16[48,64,128]{2,1,0:T(8,128)(2,1)}, u32[]{:S(2)}, u32[]{:S(2)}) %collective-permute-start.14) | collective-permute-done | bytes 786464 | tf_op jit(solution)/shard_map/ppermute | solution.py:569
  55.7 5.9 %local.1.rest_8_.sum_ref = f32[48,64,128]{2,1,0:T(8,128)} custom-call(s32[4,48]{1,0:T(4,128)S(1)} %bitcast.19, s32[1]{0:T(128)} %bitcast.7.lane_ref, bf16[48,64,128]{2,1,0:T(8,128)(2,1)S(1)} %copy-done, bf16[48,64,128]{2,1,0:T(8,128)(2,1)} %collective-permute-done.14.prev_ref, bf16[48,64,128]{2,1,0:T(8,128)(2,1)} %collective-permute-done.15.across_ref, ...), custom_call_target="tpu_custom_call" | custom-call | tf_op jit(solution)/shard_map/local/pallas_call | solution.py:262
  61.6 10.2 %all-to-all-done = bf16[64,3,48,128]{3,2,1,0:T(8,128)(2,1)S(1)} async-done(((bf16[64,3,48,128]{3,2,1,0:T(8,128)(2,1)}), bf16[64,3,48,128]{3,2,1,0:T(8,128)(2,1)S(1)}, u32[]{:S(2)}, u32[]{:S(2)}) %all-to-all-start) | async-done | bytes 2359328 | tf_op jit(solution)/shard_map/all_to_all | solution.py:563
  71.8 5.4 %first_wide.1 = (bf16[48,48,128]{2,1,0:T(8,128)(2,1)}, bf16[64,3,48,128]{3,2,1,0:T(8,128)(2,1)}) custom-call(s32[2,48]{1,0:T(2,128)} %bitcast.16, s32[3,1,64]{2,1,0:T(1,128)} %bitcast.13, s32[64]{0:T(128)} %bitcast.22, bf16[192,48,128]{2,1,0:T(8,128)(2,1)S(1)} %bitcast.11, f32[48,64,128]{2,1,0:T(8,128)} %local.1.rest_8_.sum_ref, ...), custom_call_target="tpu_custom_call" | custom-call | tf_op jit(solution)/shard_map/first_wide/pallas_call | solution.py:354
  77.3 5.5 %all-to-all-start.1 = ((bf16[64,3,48,128]{3,2,1,0:T(8,128)(2,1)}), bf16[64,3,48,128]{3,2,1,0:T(8,128)(2,1)S(1)}, u32[]{:S(2)}, u32[]{:S(2)}) async-start(bf16[64,3,48,128]{3,2,1,0:T(8,128)(2,1)} %get-tuple-element.78), calls=%async_computation.1 | async-start | bytes 4718592 | tf_op jit(solution)/shard_map/all_to_all | solution.py:563
  90.8 3.4 %collective-permute-done.1.refs_2_ = bf16[24,16,128]{2,1,0:T(8,128)(2,1)S(1)} collective-permute-done((bf16[24,16,128]{2,1,0:T(8,128)(2,1)S(1)}, bf16[24,16,128]{2,1,0:T(8,128)(2,1)S(1)}, u32[]{:S(2)}, u32[]{:S(2)}) %collective-permute-start.1) | collective-permute-done | bytes 98336 | tf_op jit(solution)/shard_map/ppermute | solution.py:516
  94.2 2.8 %collective-permute-done.2.refs_3_ = bf16[24,16,128]{2,1,0:T(8,128)(2,1)S(1)} collective-permute-done((bf16[24,16,128]{2,1,0:T(8,128)(2,1)S(1)}, bf16[24,16,128]{2,1,0:T(8,128)(2,1)S(1)}, u32[]{:S(2)}, u32[]{:S(2)}) %collective-permute-start.2) | collective-permute-done | bytes 98336 | tf_op jit(solution)/shard_map/ppermute | solution.py:516
  96.9 6.1 %collective-permute-done.3.refs_4_ = bf16[24,16,128]{2,1,0:T(8,128)(2,1)S(1)} collective-permute-done((bf16[24,16,128]{2,1,0:T(8,128)(2,1)S(1)}, bf16[24,16,128]{2,1,0:T(8,128)(2,1)S(1)}, u32[]{:S(2)}, u32[]{:S(2)}) %collective-permute-start.3) | collective-permute-done | bytes 98336 | tf_op jit(solution)/shard_map/ppermute | solution.py:516
  106.8 8.2 %collective-permute-start.10 = (bf16[24,16,128]{2,1,0:T(8,128)(2,1)}, bf16[24,16,128]{2,1,0:T(8,128)(2,1)S(1)}, u32[]{:S(2)}, u32[]{:S(2)}) collective-permute-start(bf16[24,16,128]{2,1,0:T(8,128)(2,1)} %get-tuple-element.57), channel_id=1, source_target_pairs={{0,128},{4,132},{8,136},{12,140},{16,144},{20,148},{24,152},{28,15... | collective-permute-start | bytes 294920 | tf_op jit(solution)/shard_map/ppermute | solution.py:522
  115.0 3.1 %collective-permute-start.12 = (bf16[24,16,128]{2,1,0:T(8,128)(2,1)}, bf16[24,16,128]{2,1,0:T(8,128)(2,1)S(1)}, u32[]{:S(2)}, u32[]{:S(2)}) collective-permute-start(bf16[24,16,128]{2,1,0:T(8,128)(2,1)} %get-tuple-element.59), channel_id=1, source_target_pairs={{0,192},{4,196},{8,200},{12,204},{16,208},{20,212},{24,216},{28,22... | collective-permute-start | bytes 294920 | tf_op jit(solution)/shard_map/ppermute | solution.py:522
  120.1 24.3 %collective-permute-done.10.rest_4_ = bf16[24,16,128]{2,1,0:T(8,128)(2,1)S(1)} collective-permute-done((bf16[24,16,128]{2,1,0:T(8,128)(2,1)}, bf16[24,16,128]{2,1,0:T(8,128)(2,1)S(1)}, u32[]{:S(2)}, u32[]{:S(2)}) %collective-permute-start.10) | collective-permute-done | bytes 98336 | tf_op jit(solution)/shard_map/ppermute | solution.py:522
  146.5 2.9 %collective-permute-start.9 = (bf16[24,16,128]{2,1,0:T(8,128)(2,1)}, bf16[24,16,128]{2,1,0:T(8,128)(2,1)S(1)}, u32[]{:S(2)}, u32[]{:S(2)}) collective-permute-start(bf16[24,16,128]{2,1,0:T(8,128)(2,1)} %get-tuple-element.56), channel_id=1, source_target_pairs={{0,96},{4,100},{8,104},{12,108},{16,112},{20,116},{24,120},{28,124... | collective-permute-start | bytes 294920 | tf_op jit(solution)/shard_map/ppermute | solution.py:522
  149.5 2.2 collective-permute-done.12.rest_6_
  152.5 2.5 %collective-permute-done.8.rest_2_ = bf16[24,16,128]{2,1,0:T(8,128)(2,1)S(1)} collective-permute-done((bf16[24,16,128]{2,1,0:T(8,128)(2,1)}, bf16[24,16,128]{2,1,0:T(8,128)(2,1)S(1)}, u32[]{:S(2)}, u32[]{:S(2)}) %collective-permute-start.8) | collective-permute-done | bytes 98336 | tf_op jit(solution)/shard_map/ppermute | solution.py:522
  156.4 5.9 %first_slim.1 = (bf16[48,16,128]{2,1,0:T(8,128)(2,1)}, bf16[24,16,128]{2,1,0:T(8,128)(2,1)}, bf16[24,16,128]{2,1,0:T(8,128)(2,1)}, bf16[24,16,128]{2,1,0:T(8,128...) custom-call(s32[2,48]{1,0:T(2,128)S(1)} %slim_slots.1.refs_ref, ...), custom_call_target="tpu_custom_call" | custom-call | tf_op jit(solution)/shard_map/first_slim/pallas_call | solution.py:387
  162.5 4.1 %collective-permute-start.18 = (bf16[24,16,128]{2,1,0:T(8,128)(2,1)}, bf16[24,16,128]{2,1,0:T(8,128)(2,1)S(1)}, u32[]{:S(2)}, u32[]{:S(2)}) collective-permute-start(bf16[24,16,128]{2,1,0:T(8,128)(2,1)} %get-tuple-element.63), channel_id=1, source_target_pairs={{0,8},{4,12},{8,16},{12,20},{16,24},{20,28},{24,0},{28,4},{32,40},... | collective-permute-start | bytes 294920 | tf_op jit(solution)/shard_map/ppermute | solution.py:516
  174.5 2.9 %collective-permute-done.20.refs_4_ = bf16[24,16,128]{2,1,0:T(8,128)(2,1)S(1)} collective-permute-done((bf16[24,16,128]{2,1,0:T(8,128)(2,1)}, bf16[24,16,128]{2,1,0:T(8,128)(2,1)S(1)}, u32[]{:S(2)}, u32[]{:S(2)}) %collective-permute-start.20) | collective-permute-done | bytes 98336 | tf_op jit(solution)/shard_map/ppermute | solution.py:516
  179.7 2.5 %collective-permute-done.22.refs_6_ = bf16[24,16,128]{2,1,0:T(8,128)(2,1)S(1)} collective-permute-done((bf16[24,16,128]{2,1,0:T(8,128)(2,1)}, bf16[24,16,128]{2,1,0:T(8,128)(2,1)S(1)}, u32[]{:S(2)}, u32[]{:S(2)}) %collective-permute-start.22) | collective-permute-done | bytes 98336 | tf_op jit(solution)/shard_map/ppermute | solution.py:516
  182.3 4.2 %collective-permute-done.23.refs_7_ = bf16[24,16,128]{2,1,0:T(8,128)(2,1)S(1)} collective-permute-done((bf16[24,16,128]{2,1,0:T(8,128)(2,1)}, bf16[24,16,128]{2,1,0:T(8,128)(2,1)S(1)}, u32[]{:S(2)}, u32[]{:S(2)}) %collective-permute-start.23) | collective-permute-done | bytes 98336 | tf_op jit(solution)/shard_map/ppermute | solution.py:516
  187.2 16.7 %collective-permute-done.34.rest_5_ = bf16[48,16,128]{2,1,0:T(8,128)(2,1)S(1)} collective-permute-done((bf16[48,16,128]{2,1,0:T(8,128)(2,1)}, bf16[48,16,128]{2,1,0:T(8,128)(2,1)S(1)}, u32[]{:S(2)}, u32[]{:S(2)}) %collective-permute-start.34) | collective-permute-done | bytes 196640 | tf_op jit(solution)/shard_map/ppermute | solution.py:569
  207.5 3.1 %collective-permute-start.24 = (bf16[24,16,128]{2,1,0:T(8,128)(2,1)}, bf16[24,16,128]{2,1,0:T(8,128)(2,1)S(1)}, u32[]{:S(2)}, u32[]{:S(2)}) collective-permute-start(bf16[24,16,128]{2,1,0:T(8,128)(2,1)} %get-tuple-element.71), channel_id=1, source_target_pairs={{0,32},{4,36},{8,40},{12,44},{16,48},{20,52},{24,56},{28,60},{32,6... | collective-permute-start | bytes 294920 | tf_op jit(solution)/shard_map/ppermute | solution.py:522
  213.8 3.7 %collective-permute-start.26 = (bf16[24,16,128]{2,1,0:T(8,128)(2,1)}, bf16[24,16,128]{2,1,0:T(8,128)(2,1)S(1)}, u32[]{:S(2)}, u32[]{:S(2)}) collective-permute-start(bf16[24,16,128]{2,1,0:T(8,128)(2,1)} %get-tuple-element.73), channel_id=1, source_target_pairs={{0,96},{4,100},{8,104},{12,108},{16,112},{20,116},{24,120},{28,124... | collective-permute-start | bytes 294920 | tf_op jit(solution)/shard_map/ppermute | solution.py:522
  217.4 3.1 %collective-permute-done.25.rest_2_ = bf16[24,16,128]{2,1,0:T(8,128)(2,1)S(1)} collective-permute-done((bf16[24,16,128]{2,1,0:T(8,128)(2,1)}, bf16[24,16,128]{2,1,0:T(8,128)(2,1)S(1)}, u32[]{:S(2)}, u32[]{:S(2)}) %collective-permute-start.25) | collective-permute-done | bytes 98336 | tf_op jit(solution)/shard_map/ppermute | solution.py:522
  220.5 6.5 %collective-permute-start.27 = (bf16[24,16,128]{2,1,0:T(8,128)(2,1)}, bf16[24,16,128]{2,1,0:T(8,128)(2,1)S(1)}, u32[]{:S(2)}, u32[]{:S(2)}) collective-permute-start(bf16[24,16,128]{2,1,0:T(8,128)(2,1)} %get-tuple-element.74), channel_id=1, source_target_pairs={{0,128},{4,132},{8,136},{12,140},{16,144},{20,148},{24,152},{28,15... | collective-permute-start | bytes 294920 | tf_op jit(solution)/shard_map/ppermute | solution.py:522
  227.0 4.6 %collective-permute-start.28 = (bf16[24,16,128]{2,1,0:T(8,128)(2,1)}, bf16[24,16,128]{2,1,0:T(8,128)(2,1)S(1)}, u32[]{:S(2)}, u32[]{:S(2)}) collective-permute-start(bf16[24,16,128]{2,1,0:T(8,128)(2,1)} %get-tuple-element.75), channel_id=1, source_target_pairs={{0,160},{4,164},{8,168},{12,172},{16,176},{20,180},{24,184},{28,18... | collective-permute-start | bytes 294920 | tf_op jit(solution)/shard_map/ppermute | solution.py:522
  233.3 6.3 %near.1.near_ref = f32[3,6144]{1,0:T(4,128)S(1)} custom-call(s32[4,48]{1,0:T(4,128)S(1)} %bitcast.20, s32[1]{0:T(128)} %bitcast.7.lane_ref, bf16[48,48,128]{2,1,0:T(8,128)(2,1)S(1)} %copy-done.3, bf16[48,48,128]{2,1,0:T(8,128)(2,1)S(1)} %collective-permute-done.31.rest_1_, bf16[48,48,128]{2,1,0:T(8,128)(2,1)S(1)} %collective-permute-done.32.rest_2_, ...), custom_call_target="tpu_custom_call" | custom-call | tf_op jit(solution)/shard_map/near/pallas_call | solution.py:428
  239.6 3.5 %wide.1 = (f32[3,6144]{1,0:T(4,128)S(1)}, bf16[48,2,128,128]{3,2,1,0:T(8,128)(2,1)S(1)}, bf16[48,16,128]{2,1,0:T(8,128)(2,1)S(1)}) custom-call(s32[2,48]{1,0:T(2,128)S(1)} %bitcast.18, bf16[192,48,128]{2,1,0:T(8,128)(2,1)S(1)} %bitcast.10, f32[3,6144]{1,0:T(4,128)S(1)} %near.1.near_ref, ...), custom_call_target="tpu_custom_call" | custom-call | tf_op jit(solution)/shard_map/wide/pallas_call | solution.py:462
  243.2 3.9 %moments.1 = f32[3,6144]{1,0:T(4,128)} custom-call(s32[2,48]{1,0:T(2,128)S(1)} %slim_slots.1.refs_ref, bf16[24,16,128]{2,1,0:T(8,128)(2,1)S(1)} %copy-done.7, bf16[24,16,128]{2,1,0:T(8,128)(2,1)S(1)} %collective-permute-done.24.rest_1_, bf16[24,16,128]{2,1,0:T(8,128)(2,1)S(1)} %collective-permute-done.25.rest_2_, ...), custom_call_target="tpu_custom_call" | custom-call | tf_op jit(solution)/shard_map/moments/pallas_call | solution.py:497
  (100 shorter events, 42.4 us)
Async XLA Ops:
  2.7 69.0 %all-to-all-start = ((bf16[64,3,48,128]{3,2,1,0:T(8,128)(2,1)}), bf16[64,3,48,128]{3,2,1,0:T(8,128)(2,1)S(1)}, u32[]{:S(2)}, u32[]{:S(2)}) async-start(bf16[64,3,48,128]{3,2,1,0:T(8,128)(2,1)} %pack_wide.1), calls=%async_computation | async-start | bytes 4718592 | tf_op jit(solution)/shard_map/all_to_all | solution.py:563
  17.1 36.7 %collective-permute-start.14 = (bf16[48,64,128]{2,1,0:T(8,128)(2,1)}, bf16[48,64,128]{2,1,0:T(8,128)(2,1)}, u32[]{:S(2)}, u32[]{:S(2)}) collective-permute-start(bf16[48,64,128]{2,1,0:T(8,128)(2,1)} %get-tuple-element.52.refs_8_.own_ref.rest_9_.base_ref), channel_id=1, source_target_pairs={{0,1},{1,2},{2,3},{3,0},{4,5},{5,6},{6,7},{7,4},{8,9},{9,10},{10,1... | collective-permute-start | bytes 2359304 | tf_op jit(solution)/shard_map/ppermute | solution.py:569
  18.5 35.4 %collective-permute-start.15 = (bf16[48,64,128]{2,1,0:T(8,128)(2,1)}, bf16[48,64,128]{2,1,0:T(8,128)(2,1)}, u32[]{:S(2)}, u32[]{:S(2)}) collective-permute-start(bf16[48,64,128]{2,1,0:T(8,128)(2,1)} %get-tuple-element.52.refs_8_.own_ref.rest_9_.base_ref), channel_id=1, source_target_pairs={{0,2},{1,3},{2,0},{3,1},{4,6},{5,7},{6,4},{7,5},{8,10},{9,11},{10,... | collective-permute-start | bytes 2359304 | tf_op jit(solution)/shard_map/ppermute | solution.py:569
  19.1 36.6 %collective-permute-start.16 = (bf16[48,64,128]{2,1,0:T(8,128)(2,1)}, bf16[48,64,128]{2,1,0:T(8,128)(2,1)}, u32[]{:S(2)}, u32[]{:S(2)}) collective-permute-start(bf16[48,64,128]{2,1,0:T(8,128)(2,1)} %get-tuple-element.52.refs_8_.own_ref.rest_9_.base_ref), channel_id=1, source_target_pairs={{0,3},{1,0},{2,1},{3,2},{4,7},{5,4},{6,5},{7,6},{8,11},{9,8},{10,9... | collective-permute-start | bytes 2359304 | tf_op jit(solution)/shard_map/ppermute | solution.py:569
  77.3 162.3 %all-to-all-start.1 = ((bf16[64,3,48,128]{3,2,1,0:T(8,128)(2,1)}), bf16[64,3,48,128]{3,2,1,0:T(8,128)(2,1)S(1)}, u32[]{:S(2)}, u32[]{:S(2)}) async-start(bf16[64,3,48,128]{3,2,1,0:T(8,128)(2,1)} %get-tuple-element.78), calls=%async_computation.1 | async-start | bytes 4718592 | tf_op jit(solution)/shard_map/all_to_all | solution.py:563
  82.9 11.2 %collective-permute-start.1 = (bf16[24,16,128]{2,1,0:T(8,128)(2,1)S(1)}, bf16[24,16,128]{2,1,0:T(8,128)(2,1)S(1)}, u32[]{:S(2)}, u32[]{:S(2)}) collective-permute-start(bf16[24,16,128]{2,1,0:T(8,128)(2,1)S(1)} %copy-done.19), channel_id=1, source_target_pairs={{0,8},{4,12},{8,16},{12,20},{16,24},{20,28},{24,0},{28,4},{32,40},... | collective-permute-start | bytes 294920 | tf_op jit(solution)/shard_map/ppermute | solution.py:516
  84.5 12.4 %collective-permute-start.2 = (bf16[24,16,128]{2,1,0:T(8,128)(2,1)S(1)}, bf16[24,16,128]{2,1,0:T(8,128)(2,1)S(1)}, u32[]{:S(2)}, u32[]{:S(2)}) collective-permute-start(bf16[24,16,128]{2,1,0:T(8,128)(2,1)S(1)} %copy-done.18), channel_id=1, source_target_pairs={{0,12},{4,8},{8,20},{12,16},{16,28},{20,24},{24,4},{28,0},{32,44},... | collective-permute-start | bytes 294920 | tf_op jit(solution)/shard_map/ppermute | solution.py:516
  85.7 17.3 %collective-permute-start.3 = (bf16[24,16,128]{2,1,0:T(8,128)(2,1)S(1)}, bf16[24,16,128]{2,1,0:T(8,128)(2,1)S(1)}, u32[]{:S(2)}, u32[]{:S(2)}) collective-permute-start(bf16[24,16,128]{2,1,0:T(8,128)(2,1)S(1)} %copy-done.17), channel_id=1, source_target_pairs={{0,16},{4,20},{8,24},{12,28},{16,0},{20,4},{24,8},{28,12},{32,48},... | collective-permute-start | bytes 294920 | tf_op jit(solution)/shard_map/ppermute | solution.py:516
  87.4 17.4 %collective-permute-start.4 = (bf16[24,16,128]{2,1,0:T(8,128)(2,1)S(1)}, bf16[24,16,128]{2,1,0:T(8,128)(2,1)S(1)}, u32[]{:S(2)}, u32[]{:S(2)}) collective-permute-start(bf16[24,16,128]{2,1,0:T(8,128)(2,1)S(1)} %copy-done.16), channel_id=1, source_target_pairs={{0,20},{4,16},{8,28},{12,24},{16,4},{20,0},{24,12},{28,8},{32,52},... | collective-permute-start | bytes 294920 | tf_op jit(solution)/shard_map/ppermute | solution.py:516
  89.0 15.8 %collective-permute-start.5 = (bf16[24,16,128]{2,1,0:T(8,128)(2,1)S(1)}, bf16[24,16,128]{2,1,0:T(8,128)(2,1)S(1)}, u32[]{:S(2)}, u32[]{:S(2)}) collective-permute-start(bf16[24,16,128]{2,1,0:T(8,128)(2,1)S(1)} %copy-done.15), channel_id=1, source_target_pairs={{0,24},{4,28},{8,0},{12,4},{16,8},{20,12},{24,16},{28,20},{32,56},... | collective-permute-start | bytes 294920 | tf_op jit(solution)/shard_map/ppermute | solution.py:516
  94.2 10.7 %collective-permute-start.6 = (bf16[24,16,128]{2,1,0:T(8,128)(2,1)S(1)}, bf16[24,16,128]{2,1,0:T(8,128)(2,1)S(1)}, u32[]{:S(2)}, u32[]{:S(2)}) collective-permute-start(bf16[24,16,128]{2,1,0:T(8,128)(2,1)S(1)} %copy-done.14), channel_id=1, source_target_pairs={{0,28},{4,24},{8,4},{12,0},{16,12},{20,8},{24,20},{28,16},{32,60},... | collective-permute-start | bytes 294920 | tf_op jit(solution)/shard_map/ppermute | solution.py:516
  106.8 37.6 %collective-permute-start.10 = (bf16[24,16,128]{2,1,0:T(8,128)(2,1)}, bf16[24,16,128]{2,1,0:T(8,128)(2,1)S(1)}, u32[]{:S(2)}, u32[]{:S(2)}) collective-permute-start(bf16[24,16,128]{2,1,0:T(8,128)(2,1)} %get-tuple-element.57), channel_id=1, source_target_pairs={{0,128},{4,132},{8,136},{12,140},{16,144},{20,148},{24,152},{28,15... | collective-permute-start | bytes 294920 | tf_op jit(solution)/shard_map/ppermute | solution.py:522
  115.0 31.5 %collective-permute-start.11 = (bf16[24,16,128]{2,1,0:T(8,128)(2,1)}, bf16[24,16,128]{2,1,0:T(8,128)(2,1)S(1)}, u32[]{:S(2)}, u32[]{:S(2)}) collective-permute-start(bf16[24,16,128]{2,1,0:T(8,128)(2,1)} %get-tuple-element.58), channel_id=1, source_target_pairs={{0,160},{4,164},{8,168},{12,172},{16,176},{20,180},{24,184},{28,18... | collective-permute-start | bytes 294920 | tf_op jit(solution)/shard_map/ppermute | solution.py:522
  115.0 36.7 %collective-permute-start.12 = (bf16[24,16,128]{2,1,0:T(8,128)(2,1)}, bf16[24,16,128]{2,1,0:T(8,128)(2,1)S(1)}, u32[]{:S(2)}, u32[]{:S(2)}) collective-permute-start(bf16[24,16,128]{2,1,0:T(8,128)(2,1)} %get-tuple-element.59), channel_id=1, source_target_pairs={{0,192},{4,196},{8,200},{12,204},{16,208},{20,212},{24,216},{28,22... | collective-permute-start | bytes 294920 | tf_op jit(solution)/shard_map/ppermute | solution.py:522
  118.1 34.5 %collective-permute-start.13 = (bf16[24,16,128]{2,1,0:T(8,128)(2,1)}, bf16[24,16,128]{2,1,0:T(8,128)(2,1)S(1)}, u32[]{:S(2)}, u32[]{:S(2)}) collective-permute-start(bf16[24,16,128]{2,1,0:T(8,128)(2,1)} %get-tuple-element.60), channel_id=1, source_target_pairs={{0,224},{4,228},{8,232},{12,236},{16,240},{20,244},{24,248},{28,25... | collective-permute-start | bytes 294920 | tf_op jit(solution)/shard_map/ppermute | solution.py:522
  119.6 33.0 %collective-permute-start.7 = (bf16[24,16,128]{2,1,0:T(8,128)(2,1)}, bf16[24,16,128]{2,1,0:T(8,128)(2,1)S(1)}, u32[]{:S(2)}, u32[]{:S(2)}) collective-permute-start(bf16[24,16,128]{2,1,0:T(8,128)(2,1)} %get-tuple-element.54), channel_id=1, source_target_pairs={{0,32},{4,36},{8,40},{12,44},{16,48},{20,52},{24,56},{28,60},{32,6... | collective-permute-start | bytes 294920 | tf_op jit(solution)/shard_map/ppermute | solution.py:522
  144.4 10.7 %collective-permute-start.8 = (bf16[24,16,128]{2,1,0:T(8,128)(2,1)}, bf16[24,16,128]{2,1,0:T(8,128)(2,1)S(1)}, u32[]{:S(2)}, u32[]{:S(2)}) collective-permute-start(bf16[24,16,128]{2,1,0:T(8,128)(2,1)} %get-tuple-element.55), channel_id=1, source_target_pairs={{0,64},{4,68},{8,72},{12,76},{16,80},{20,84},{24,88},{28,92},{32,9... | collective-permute-start | bytes 294920 | tf_op jit(solution)/shard_map/ppermute | solution.py:522
  146.5 9.0 %collective-permute-start.9 = (bf16[24,16,128]{2,1,0:T(8,128)(2,1)}, bf16[24,16,128]{2,1,0:T(8,128)(2,1)S(1)}, u32[]{:S(2)}, u32[]{:S(2)}) collective-permute-start(bf16[24,16,128]{2,1,0:T(8,128)(2,1)} %get-tuple-element.56), channel_id=1, source_target_pairs={{0,96},{4,100},{8,104},{12,108},{16,112},{20,116},{24,120},{28,124... | collective-permute-start | bytes 294920 | tf_op jit(solution)/shard_map/ppermute | solution.py:522
  162.5 9.6 %collective-permute-start.18 = (bf16[24,16,128]{2,1,0:T(8,128)(2,1)}, bf16[24,16,128]{2,1,0:T(8,128)(2,1)S(1)}, u32[]{:S(2)}, u32[]{:S(2)}) collective-permute-start(bf16[24,16,128]{2,1,0:T(8,128)(2,1)} %get-tuple-element.63), channel_id=1, source_target_pairs={{0,8},{4,12},{8,16},{12,20},{16,24},{20,28},{24,0},{28,4},{32,40},... | collective-permute-start | bytes 294920 | tf_op jit(solution)/shard_map/ppermute | solution.py:516
  167.6 9.9 %collective-permute-start.20 = (bf16[24,16,128]{2,1,0:T(8,128)(2,1)}, bf16[24,16,128]{2,1,0:T(8,128)(2,1)S(1)}, u32[]{:S(2)}, u32[]{:S(2)}) collective-permute-start(bf16[24,16,128]{2,1,0:T(8,128)(2,1)} %get-tuple-element.65), channel_id=1, source_target_pairs={{0,16},{4,20},{8,24},{12,28},{16,0},{20,4},{24,8},{28,12},{32,48},... | collective-permute-start | bytes 294920 | tf_op jit(solution)/shard_map/ppermute | solution.py:516
  169.4 9.0 %collective-permute-start.21 = (bf16[24,16,128]{2,1,0:T(8,128)(2,1)}, bf16[24,16,128]{2,1,0:T(8,128)(2,1)S(1)}, u32[]{:S(2)}, u32[]{:S(2)}) collective-permute-start(bf16[24,16,128]{2,1,0:T(8,128)(2,1)} %get-tuple-element.66), channel_id=1, source_target_pairs={{0,20},{4,16},{8,28},{12,24},{16,4},{20,0},{24,12},{28,8},{32,52},... | collective-permute-start | bytes 294920 | tf_op jit(solution)/shard_map/ppermute | solution.py:516
  170.8 56.2 %collective-permute-start.31 = (bf16[48,48,128]{2,1,0:T(8,128)(2,1)S(1)}, bf16[48,48,128]{2,1,0:T(8,128)(2,1)S(1)}, u32[]{:S(2)}, u32[]{:S(2)}) collective-permute-start(bf16[48,48,128]{2,1,0:T(8,128)(2,1)S(1)} %copy-done.3), channel_id=1, source_target_pairs={{0,1},{1,2},{2,3},{3,0},{4,5},{5,6},{6,7},{7,4},{8,9},{9,10},{10,1... | collective-permute-start | bytes 1769480 | tf_op jit(solution)/shard_map/ppermute | solution.py:569
  172.1 59.6 %collective-permute-start.32 = (bf16[48,48,128]{2,1,0:T(8,128)(2,1)S(1)}, bf16[48,48,128]{2,1,0:T(8,128)(2,1)S(1)}, u32[]{:S(2)}, u32[]{:S(2)}) collective-permute-start(bf16[48,48,128]{2,1,0:T(8,128)(2,1)S(1)} %copy-done.3), channel_id=1, source_target_pairs={{0,2},{1,3},{2,0},{3,1},{4,6},{5,7},{6,4},{7,5},{8,10},{9,11},{10,... | collective-permute-start | bytes 1769480 | tf_op jit(solution)/shard_map/ppermute | solution.py:569
  173.3 58.4 %collective-permute-start.33 = (bf16[48,48,128]{2,1,0:T(8,128)(2,1)S(1)}, bf16[48,48,128]{2,1,0:T(8,128)(2,1)S(1)}, u32[]{:S(2)}, u32[]{:S(2)}) collective-permute-start(bf16[48,48,128]{2,1,0:T(8,128)(2,1)S(1)} %copy-done.3), channel_id=1, source_target_pairs={{0,3},{1,0},{2,1},{3,2},{4,7},{5,4},{6,5},{7,6},{8,11},{9,8},{10,9... | collective-permute-start | bytes 1769480 | tf_op jit(solution)/shard_map/ppermute | solution.py:569
  178.5 25.4 %collective-permute-start.34 = (bf16[48,16,128]{2,1,0:T(8,128)(2,1)}, bf16[48,16,128]{2,1,0:T(8,128)(2,1)S(1)}, u32[]{:S(2)}, u32[]{:S(2)}) collective-permute-start(bf16[48,16,128]{2,1,0:T(8,128)(2,1)} %get-tuple-element.69.refs_8_.rest_4_), channel_id=1, source_target_pairs={{0,1},{1,2},{2,3},{3,0},{4,5},{5,6},{6,7},{7,4},{8,9},{9,10},{10,1... | collective-permute-start | bytes 589832 | tf_op jit(solution)/shard_map/ppermute | solution.py:569
  186.5 21.0 %collective-permute-start.35 = (bf16[48,16,128]{2,1,0:T(8,128)(2,1)}, bf16[48,16,128]{2,1,0:T(8,128)(2,1)S(1)}, u32[]{:S(2)}, u32[]{:S(2)}) collective-permute-start(bf16[48,16,128]{2,1,0:T(8,128)(2,1)} %get-tuple-element.69.refs_8_.rest_4_), channel_id=1, source_target_pairs={{0,2},{1,3},{2,0},{3,1},{4,6},{5,7},{6,4},{7,5},{8,10},{9,11},{10,... | collective-permute-start | bytes 589832 | tf_op jit(solution)/shard_map/ppermute | solution.py:569
  210.7 9.9 %collective-permute-start.25 = (bf16[24,16,128]{2,1,0:T(8,128)(2,1)}, bf16[24,16,128]{2,1,0:T(8,128)(2,1)S(1)}, u32[]{:S(2)}, u32[]{:S(2)}) collective-permute-start(bf16[24,16,128]{2,1,0:T(8,128)(2,1)} %get-tuple-element.72), channel_id=1, source_target_pairs={{0,64},{4,68},{8,72},{12,76},{16,80},{20,84},{24,88},{28,92},{32,9... | collective-permute-start | bytes 294920 | tf_op jit(solution)/shard_map/ppermute | solution.py:522
  213.8 29.4 %collective-permute-start.26 = (bf16[24,16,128]{2,1,0:T(8,128)(2,1)}, bf16[24,16,128]{2,1,0:T(8,128)(2,1)S(1)}, u32[]{:S(2)}, u32[]{:S(2)}) collective-permute-start(bf16[24,16,128]{2,1,0:T(8,128)(2,1)} %get-tuple-element.73), channel_id=1, source_target_pairs={{0,96},{4,100},{8,104},{12,108},{16,112},{20,116},{24,120},{28,124... | collective-permute-start | bytes 294920 | tf_op jit(solution)/shard_map/ppermute | solution.py:522
  220.5 22.6 %collective-permute-start.27 = (bf16[24,16,128]{2,1,0:T(8,128)(2,1)}, bf16[24,16,128]{2,1,0:T(8,128)(2,1)S(1)}, u32[]{:S(2)}, u32[]{:S(2)}) collective-permute-start(bf16[24,16,128]{2,1,0:T(8,128)(2,1)} %get-tuple-element.74), channel_id=1, source_target_pairs={{0,128},{4,132},{8,136},{12,140},{16,144},{20,148},{24,152},{28,15... | collective-permute-start | bytes 294920 | tf_op jit(solution)/shard_map/ppermute | solution.py:522
  227.0 16.1 %collective-permute-start.28 = (bf16[24,16,128]{2,1,0:T(8,128)(2,1)}, bf16[24,16,128]{2,1,0:T(8,128)(2,1)S(1)}, u32[]{:S(2)}, u32[]{:S(2)}) collective-permute-start(bf16[24,16,128]{2,1,0:T(8,128)(2,1)} %get-tuple-element.75), channel_id=1, source_target_pairs={{0,160},{4,164},{8,168},{12,172},{16,176},{20,180},{24,184},{28,18... | collective-permute-start | bytes 294920 | tf_op jit(solution)/shard_map/ppermute | solution.py:522
  231.7 11.5 %collective-permute-start.29 = (bf16[24,16,128]{2,1,0:T(8,128)(2,1)}, bf16[24,16,128]{2,1,0:T(8,128)(2,1)S(1)}, u32[]{:S(2)}, u32[]{:S(2)}) collective-permute-start(bf16[24,16,128]{2,1,0:T(8,128)(2,1)} %get-tuple-element.76), channel_id=1, source_target_pairs={{0,192},{4,196},{8,200},{12,204},{16,208},{20,212},{24,216},{28,22... | collective-permute-start | bytes 294920 | tf_op jit(solution)/shard_map/ppermute | solution.py:522
  231.7 11.5 %collective-permute-start.30 = (bf16[24,16,128]{2,1,0:T(8,128)(2,1)}, bf16[24,16,128]{2,1,0:T(8,128)(2,1)S(1)}, u32[]{:S(2)}, u32[]{:S(2)}) collective-permute-start(bf16[24,16,128]{2,1,0:T(8,128)(2,1)} %get-tuple-element.77), channel_id=1, source_target_pairs={{0,224},{4,228},{8,232},{12,236},{16,240},{20,244},{24,248},{28,25... | collective-permute-start | bytes 294920 | tf_op jit(solution)/shard_map/ppermute | solution.py:522
  (28 other events, 494.4 us)
where the time goes:
time: 248 us; the launch traced here: 247 us
  waiting for transfers between devices  122 us (49%)
  starting transfers between devices  79.5 us (32%)
  Pallas kernels  42.6 us (17%)
  local copies, waits for them, and re-layouts  2.8 us (1%)
    ppermute x9, waiting for transfers between devices, panel(): lax.ppermute(own, 'grp', [(i, (i + shift) % LANES) for i in range(LANES)])  49.7 us
    ppermute x14, starting transfers between devices, along_z(): lax.ppermute(sends[dz], 'dom', [(i, (i + dz * PLANE) % size) for i in ran...  37 us
    ppermute x14, waiting for transfers between devices, along_z(): lax.ppermute(sends[dz], 'dom', [(i, (i + dz * PLANE) % size) for i in ran...  36.5 us
    ppermute x14, waiting for transfers between devices, across_plane(): lax.ppermute(sends[k], 'dom', [(i, plane_step(i, k)) for i in range(size)])  25.4 us
    all_to_all x2, starting transfers between devices, exchange(): got = lax.all_to_all(send, 'dom', split_axis=0, concat_axis=0, tiled=True)  17.6 us
    ppermute x14, starting transfers between devices, across_plane(): lax.ppermute(sends[k], 'dom', [(i, plane_step(i, k)) for i in range(size)])  16.4 us
    all_to_all x2, waiting for transfers between devices, exchange(): got = lax.all_to_all(send, 'dom', split_axis=0, concat_axis=0, tiled=True)  10.2 us
    ppermute x9, starting transfers between devices, panel(): lax.ppermute(own, 'grp', [(i, (i + shift) % LANES) for i in range(LANES)])  8.57 us
  transfers between devices with their start and end apart: 39, of which 22 were waited for; matrix products, arithmetic and copies ran while one was open for 0% of the time, Pallas kernels for 12%

commit v1 on v0

--- a/solution.py
+++ b/solution.py
@@ -399,7 +399,7 @@
         out_shape=[pltpu.HBM((rows, slim, size), kind)] + slim_shapes(peers, slots, slim, size, kind),
         compiler_params=grant(24),
         name="first_slim",
-    )(refs, table, counts, me, *got, in_hbm(sums), in_hbm(blocks))
+    )(in_hbm(refs), in_hbm(table), in_hbm(counts), me, *got, in_hbm(sums), in_hbm(blocks))
 
 
 def near_kernel(scale, cols_ref, lane_ref, *rest):
@@ -502,7 +502,7 @@
         out_shape=jax.ShapeDtypeStruct(near.shape, near.dtype),
         compiler_params=grant(24),
         name="moments",
-    )(refs, *got, in_vmem(near), in_vmem(far), in_vmem(base))
+    )(in_hbm(refs), *got, in_vmem(near), in_vmem(far), in_vmem(base))
 
 
 def plane_step(i, k):
@@ -588,7 +588,7 @@
     sides = across_plane(sides)
     pieces = pieces + panel(slim_first)
     sides = turn(sides, slim_first)
-    slim = {0: sides[0]} | along_z(sides, (4, 3, 5, 2, 6, 1, 7))
+    slim = {0: sides[0]} | along_z(sides, (4, 3, 5, 2, 6, 7, 1))
     slim = [slim[dz] for dz in range(ZS)]
     near = near_part(cols, lane, pieces, blocks, base, scale[:2] + (None,))
     near, far, rest = wide_part(refs, wide, near, base, blocks)

time: 248 us -> 248 us (level)
  no operation moved by 1% of the time
where the time goes in v1:
time: 248 us
  waiting for transfers between devices  121 us (49%)
  starting transfers between devices  79.5 us (32%)
  Pallas kernels  43 us (17%)
  local copies, waits for them, and re-layouts  3.37 us (1%)
    ppermute x9, waiting for transfers between devices, panel(): lax.ppermute(own, 'grp', [(i, (i + shift) % LANES) for i in range(LANES)])  49.7 us
    ppermute x14, starting transfers between devices, along_z(): lax.ppermute(sends[dz], 'dom', [(i, (i + dz * PLANE) % size) for i in ran...  37 us
    ppermute x14, waiting for transfers between devices, along_z(): lax.ppermute(sends[dz], 'dom', [(i, (i + dz * PLANE) % size) for i in ran...  35.9 us
    ppermute x14, waiting for transfers between devices, across_plane(): lax.ppermute(sends[k], 'dom', [(i, plane_step(i, k)) for i in range(size)])  25.4 us
    all_to_all x2, starting transfers between devices, exchange(): got = lax.all_to_all(send, 'dom', split_axis=0, concat_axis=0, tiled=True)  17.6 us
    ppermute x14, starting transfers between devices, across_plane(): lax.ppermute(sends[k], 'dom', [(i, plane_step(i, k)) for i in range(size)])  16.4 us
    all_to_all x2, waiting for transfers between devices, exchange(): got = lax.all_to_all(send, 'dom', split_axis=0, concat_axis=0, tiled=True)  10.2 us
    ppermute x9, starting transfers between devices, panel(): lax.ppermute(own, 'grp', [(i, (i + shift) % LANES) for i in range(LANES)])  8.55 us
  transfers between devices with their start and end apart: 39, of which 22 were waited for; matrix products, arithmetic and copies ran while one was open for 0% of the time, Pallas kernels for 12%

profile of v1, /device:TPU:16, one launch (start us, length us, event | category | flops | bytes accessed | tf_op | source)
XLA Modules:
  0.0 247.7 jit_solution(1371368418145774135)
XLA Ops:
  0.0 2.7 %pack_wide.1 = bf16[64,3,48,128]{3,2,1,0:T(8,128)(2,1)} custom-call(s32[3,1,64]{2,1,0:T(1,128)} %bitcast.12, s32[64]{0:T(128)} %bitcast.21, bf16[64,6144]{1,0:T(8,128)(2,1)} %probes_ref.3), custom_call_target="tpu_custom_call" | custom-call | tf_op jit(solution)/shard_map/pack_wide/pallas_call | solution.py:100
  2.7 12.1 %all-to-all-start = ((bf16[64,3,48,128]{3,2,1,0:T(8,128)(2,1)}), bf16[64,3,48,128]{3,2,1,0:T(8,128)(2,1)S(1)}, u32[]{:S(2)}, u32[]{:S(2)}) async-start(bf16[64,3,48,128]{3,2,1,0:T(8,128)(2,1)} %pack_wide.1), calls=%async_computation | async-start | bytes 4718592 | tf_op jit(solution)/shard_map/all_to_all | solution.py:563
  14.8 2.3 pack_slim.1
  20.2 2.9 %fetch.1.close_ref = bf16[48,4,128,128]{3,2,1,0:T(8,128)(2,1)S(1)} custom-call(bf16[48,6,128,128]{3,2,1,0:T(8,128)(2,1)} %blocks_ref.5), custom_call_target="tpu_custom_call" | custom-call | tf_op jit(solution)/shard_map/fetch/pallas_call | solution.py:181
  23.0 30.8 %collective-permute-done.14.prev_ref = bf16[48,64,128]{2,1,0:T(8,128)(2,1)} collective-permute-done((bf16[48,64,128]{2,1,0:T(8,128)(2,1)}, bf16[48,64,128]{2,1,0:T(8,128)(2,1)}, u32[]{:S(2)}, u32[]{:S(2)}) %collective-permute-start.14) | collective-permute-done | bytes 786464 | tf_op jit(solution)/shard_map/ppermute | solution.py:569
  55.7 5.8 %local.1.rest_8_.sum_ref = f32[48,64,128]{2,1,0:T(8,128)} custom-call(s32[4,48]{1,0:T(4,128)S(1)} %bitcast.19, s32[1]{0:T(128)} %bitcast.7.lane_ref, bf16[48,64,128]{2,1,0:T(8,128)(2,1)S(1)} %copy-done, bf16[48,64,128]{2,1,0:T(8,128)(2,1)} %collective-permute-done.14.prev_ref, bf16[48,64,128]{2,1,0:T(8,128)(2,1)} %collective-permute-done.15.across_ref, ...), custom_call_target="tpu_custom_call" | custom-call | tf_op jit(solution)/shard_map/local/pallas_call | solution.py:262
  61.6 10.2 %all-to-all-done = bf16[64,3,48,128]{3,2,1,0:T(8,128)(2,1)S(1)} async-done(((bf16[64,3,48,128]{3,2,1,0:T(8,128)(2,1)}), bf16[64,3,48,128]{3,2,1,0:T(8,128)(2,1)S(1)}, u32[]{:S(2)}, u32[]{:S(2)}) %all-to-all-start) | async-done | bytes 2359328 | tf_op jit(solution)/shard_map/all_to_all | solution.py:563
  71.8 5.4 %first_wide.1 = (bf16[48,48,128]{2,1,0:T(8,128)(2,1)}, bf16[64,3,48,128]{3,2,1,0:T(8,128)(2,1)}) custom-call(s32[2,48]{1,0:T(2,128)} %bitcast.16, s32[3,1,64]{2,1,0:T(1,128)} %bitcast.13, s32[64]{0:T(128)} %bitcast.22, bf16[192,48,128]{2,1,0:T(8,128)(2,1)S(1)} %bitcast.11, f32[48,64,128]{2,1,0:T(8,128)} %local.1.rest_8_.sum_ref, ...), custom_call_target="tpu_custom_call" | custom-call | tf_op jit(solution)/shard_map/first_wide/pallas_call | solution.py:354
  77.2 5.5 %all-to-all-start.1 = ((bf16[64,3,48,128]{3,2,1,0:T(8,128)(2,1)}), bf16[64,3,48,128]{3,2,1,0:T(8,128)(2,1)S(1)}, u32[]{:S(2)}, u32[]{:S(2)}) async-start(bf16[64,3,48,128]{3,2,1,0:T(8,128)(2,1)} %get-tuple-element.78), calls=%async_computation.1 | async-start | bytes 4718592 | tf_op jit(solution)/shard_map/all_to_all | solution.py:563
  90.7 3.4 %collective-permute-done.1.refs_2_ = bf16[24,16,128]{2,1,0:T(8,128)(2,1)S(1)} collective-permute-done((bf16[24,16,128]{2,1,0:T(8,128)(2,1)S(1)}, bf16[24,16,128]{2,1,0:T(8,128)(2,1)S(1)}, u32[]{:S(2)}, u32[]{:S(2)}) %collective-permute-start.1) | collective-permute-done | bytes 98336 | tf_op jit(solution)/shard_map/ppermute | solution.py:516
  94.1 2.8 %collective-permute-done.2.refs_3_ = bf16[24,16,128]{2,1,0:T(8,128)(2,1)S(1)} collective-permute-done((bf16[24,16,128]{2,1,0:T(8,128)(2,1)S(1)}, bf16[24,16,128]{2,1,0:T(8,128)(2,1)S(1)}, u32[]{:S(2)}, u32[]{:S(2)}) %collective-permute-start.2) | collective-permute-done | bytes 98336 | tf_op jit(solution)/shard_map/ppermute | solution.py:516
  96.9 6.1 %collective-permute-done.3.refs_4_ = bf16[24,16,128]{2,1,0:T(8,128)(2,1)S(1)} collective-permute-done((bf16[24,16,128]{2,1,0:T(8,128)(2,1)S(1)}, bf16[24,16,128]{2,1,0:T(8,128)(2,1)S(1)}, u32[]{:S(2)}, u32[]{:S(2)}) %collective-permute-start.3) | collective-permute-done | bytes 98336 | tf_op jit(solution)/shard_map/ppermute | solution.py:516
  104.8 2.0 turn.2
  106.8 8.2 %collective-permute-start.10 = (bf16[24,16,128]{2,1,0:T(8,128)(2,1)}, bf16[24,16,128]{2,1,0:T(8,128)(2,1)S(1)}, u32[]{:S(2)}, u32[]{:S(2)}) collective-permute-start(bf16[24,16,128]{2,1,0:T(8,128)(2,1)} %get-tuple-element.57), channel_id=1, source_target_pairs={{0,128},{4,132},{8,136},{12,140},{16,144},{20,148},{24,152},{28,15... | collective-permute-start | bytes 294920 | tf_op jit(solution)/shard_map/ppermute | solution.py:522
  115.0 3.1 %collective-permute-start.12 = (bf16[24,16,128]{2,1,0:T(8,128)(2,1)}, bf16[24,16,128]{2,1,0:T(8,128)(2,1)S(1)}, u32[]{:S(2)}, u32[]{:S(2)}) collective-permute-start(bf16[24,16,128]{2,1,0:T(8,128)(2,1)} %get-tuple-element.59), channel_id=1, source_target_pairs={{0,192},{4,196},{8,200},{12,204},{16,208},{20,212},{24,216},{28,22... | collective-permute-start | bytes 294920 | tf_op jit(solution)/shard_map/ppermute | solution.py:522
  120.1 24.3 %collective-permute-done.10.rest_4_ = bf16[24,16,128]{2,1,0:T(8,128)(2,1)S(1)} collective-permute-done((bf16[24,16,128]{2,1,0:T(8,128)(2,1)}, bf16[24,16,128]{2,1,0:T(8,128)(2,1)S(1)}, u32[]{:S(2)}, u32[]{:S(2)}) %collective-permute-start.10) | collective-permute-done | bytes 98336 | tf_op jit(solution)/shard_map/ppermute | solution.py:522
  146.5 2.9 %collective-permute-start.9 = (bf16[24,16,128]{2,1,0:T(8,128)(2,1)}, bf16[24,16,128]{2,1,0:T(8,128)(2,1)S(1)}, u32[]{:S(2)}, u32[]{:S(2)}) collective-permute-start(bf16[24,16,128]{2,1,0:T(8,128)(2,1)} %get-tuple-element.56), channel_id=1, source_target_pairs={{0,96},{4,100},{8,104},{12,108},{16,112},{20,116},{24,120},{28,124... | collective-permute-start | bytes 294920 | tf_op jit(solution)/shard_map/ppermute | solution.py:522
  152.5 2.5 %collective-permute-done.8.rest_2_ = bf16[24,16,128]{2,1,0:T(8,128)(2,1)S(1)} collective-permute-done((bf16[24,16,128]{2,1,0:T(8,128)(2,1)}, bf16[24,16,128]{2,1,0:T(8,128)(2,1)S(1)}, u32[]{:S(2)}, u32[]{:S(2)}) %collective-permute-start.8) | collective-permute-done | bytes 98336 | tf_op jit(solution)/shard_map/ppermute | solution.py:522
  156.4 6.2 %first_slim.1 = (bf16[48,16,128]{2,1,0:T(8,128)(2,1)}, bf16[24,16,128]{2,1,0:T(8,128)(2,1)}, bf16[24,16,128]{2,1,0:T(8,128)(2,1)}, bf16[24,16,128]{2,1,0:T(8,128...) custom-call(s32[2,48]{1,0:T(2,128)} %copy-done.10, ...), custom_call_target="tpu_custom_call" | custom-call | tf_op jit(solution)/shard_map/first_slim/pallas_call | solution.py:387
  162.7 4.1 %collective-permute-start.18 = (bf16[24,16,128]{2,1,0:T(8,128)(2,1)}, bf16[24,16,128]{2,1,0:T(8,128)(2,1)S(1)}, u32[]{:S(2)}, u32[]{:S(2)}) collective-permute-start(bf16[24,16,128]{2,1,0:T(8,128)(2,1)} %get-tuple-element.63), channel_id=1, source_target_pairs={{0,8},{4,12},{8,16},{12,20},{16,24},{20,28},{24,0},{28,4},{32,40},... | collective-permute-start | bytes 294920 | tf_op jit(solution)/shard_map/ppermute | solution.py:516
  174.8 2.9 %collective-permute-done.20.refs_4_ = bf16[24,16,128]{2,1,0:T(8,128)(2,1)S(1)} collective-permute-done((bf16[24,16,128]{2,1,0:T(8,128)(2,1)}, bf16[24,16,128]{2,1,0:T(8,128)(2,1)S(1)}, u32[]{:S(2)}, u32[]{:S(2)}) %collective-permute-start.20) | collective-permute-done | bytes 98336 | tf_op jit(solution)/shard_map/ppermute | solution.py:516
  180.0 2.5 %collective-permute-done.22.refs_6_ = bf16[24,16,128]{2,1,0:T(8,128)(2,1)S(1)} collective-permute-done((bf16[24,16,128]{2,1,0:T(8,128)(2,1)}, bf16[24,16,128]{2,1,0:T(8,128)(2,1)S(1)}, u32[]{:S(2)}, u32[]{:S(2)}) %collective-permute-start.22) | collective-permute-done | bytes 98336 | tf_op jit(solution)/shard_map/ppermute | solution.py:516
  182.5 4.2 %collective-permute-done.23.refs_7_ = bf16[24,16,128]{2,1,0:T(8,128)(2,1)S(1)} collective-permute-done((bf16[24,16,128]{2,1,0:T(8,128)(2,1)}, bf16[24,16,128]{2,1,0:T(8,128)(2,1)S(1)}, u32[]{:S(2)}, u32[]{:S(2)}) %collective-permute-start.23) | collective-permute-done | bytes 98336 | tf_op jit(solution)/shard_map/ppermute | solution.py:516
  187.4 16.7 %collective-permute-done.34.rest_5_ = bf16[48,16,128]{2,1,0:T(8,128)(2,1)S(1)} collective-permute-done((bf16[48,16,128]{2,1,0:T(8,128)(2,1)}, bf16[48,16,128]{2,1,0:T(8,128)(2,1)S(1)}, u32[]{:S(2)}, u32[]{:S(2)}) %collective-permute-start.34) | collective-permute-done | bytes 196640 | tf_op jit(solution)/shard_map/ppermute | solution.py:569
  207.8 3.1 %collective-permute-start.24 = (bf16[24,16,128]{2,1,0:T(8,128)(2,1)}, bf16[24,16,128]{2,1,0:T(8,128)(2,1)S(1)}, u32[]{:S(2)}, u32[]{:S(2)}) collective-permute-start(bf16[24,16,128]{2,1,0:T(8,128)(2,1)} %get-tuple-element.71), channel_id=1, source_target_pairs={{0,32},{4,36},{8,40},{12,44},{16,48},{20,52},{24,56},{28,60},{32,6... | collective-permute-start | bytes 294920 | tf_op jit(solution)/shard_map/ppermute | solution.py:522
  214.0 3.7 %collective-permute-start.26 = (bf16[24,16,128]{2,1,0:T(8,128)(2,1)}, bf16[24,16,128]{2,1,0:T(8,128)(2,1)S(1)}, u32[]{:S(2)}, u32[]{:S(2)}) collective-permute-start(bf16[24,16,128]{2,1,0:T(8,128)(2,1)} %get-tuple-element.73), channel_id=1, source_target_pairs={{0,96},{4,100},{8,104},{12,108},{16,112},{20,116},{24,120},{28,124... | collective-permute-start | bytes 294920 | tf_op jit(solution)/shard_map/ppermute | solution.py:522
  217.7 3.1 %collective-permute-done.25.rest_2_ = bf16[24,16,128]{2,1,0:T(8,128)(2,1)S(1)} collective-permute-done((bf16[24,16,128]{2,1,0:T(8,128)(2,1)}, bf16[24,16,128]{2,1,0:T(8,128)(2,1)S(1)}, u32[]{:S(2)}, u32[]{:S(2)}) %collective-permute-start.25) | collective-permute-done | bytes 98336 | tf_op jit(solution)/shard_map/ppermute | solution.py:522
  220.8 6.6 %collective-permute-start.27 = (bf16[24,16,128]{2,1,0:T(8,128)(2,1)}, bf16[24,16,128]{2,1,0:T(8,128)(2,1)S(1)}, u32[]{:S(2)}, u32[]{:S(2)}) collective-permute-start(bf16[24,16,128]{2,1,0:T(8,128)(2,1)} %get-tuple-element.74), channel_id=1, source_target_pairs={{0,128},{4,132},{8,136},{12,140},{16,144},{20,148},{24,152},{28,15... | collective-permute-start | bytes 294920 | tf_op jit(solution)/shard_map/ppermute | solution.py:522
  227.4 4.6 %collective-permute-start.28 = (bf16[24,16,128]{2,1,0:T(8,128)(2,1)}, bf16[24,16,128]{2,1,0:T(8,128)(2,1)S(1)}, u32[]{:S(2)}, u32[]{:S(2)}) collective-permute-start(bf16[24,16,128]{2,1,0:T(8,128)(2,1)} %get-tuple-element.75), channel_id=1, source_target_pairs={{0,160},{4,164},{8,168},{12,172},{16,176},{20,180},{24,184},{28,18... | collective-permute-start | bytes 294920 | tf_op jit(solution)/shard_map/ppermute | solution.py:522
  233.5 6.3 %near.1.near_ref = f32[3,6144]{1,0:T(4,128)S(1)} custom-call(s32[4,48]{1,0:T(4,128)S(1)} %bitcast.20, s32[1]{0:T(128)} %bitcast.7.lane_ref, bf16[48,48,128]{2,1,0:T(8,128)(2,1)S(1)} %copy-done.3, bf16[48,48,128]{2,1,0:T(8,128)(2,1)S(1)} %collective-permute-done.31.rest_1_, bf16[48,48,128]{2,1,0:T(8,128)(2,1)S(1)} %collective-permute-done.32.rest_2_, ...), custom_call_target="tpu_custom_call" | custom-call | tf_op jit(solution)/shard_map/near/pallas_call | solution.py:428
  239.9 3.5 %wide.1 = (f32[3,6144]{1,0:T(4,128)S(1)}, bf16[48,2,128,128]{3,2,1,0:T(8,128)(2,1)S(1)}, bf16[48,16,128]{2,1,0:T(8,128)(2,1)S(1)}) custom-call(s32[2,48]{1,0:T(2,128)S(1)} %bitcast.18, bf16[192,48,128]{2,1,0:T(8,128)(2,1)S(1)} %bitcast.10, f32[3,6144]{1,0:T(4,128)S(1)} %near.1.near_ref, ...), custom_call_target="tpu_custom_call" | custom-call | tf_op jit(solution)/shard_map/wide/pallas_call | solution.py:462
  243.5 4.0 %moments.1 = f32[3,6144]{1,0:T(4,128)} custom-call(s32[2,48]{1,0:T(2,128)} %copy-done.10, bf16[24,16,128]{2,1,0:T(8,128)(2,1)S(1)} %copy-done.7, bf16[24,16,128]{2,1,0:T(8,128)(2,1)S(1)} %collective-permute-done.24.rest_1_, bf16[24,16,128]{2,1,0:T(8,128)(2,1)S(1)} %collective-permute-done.25.rest_2_, ...), custom_call_target="tpu_custom_call" | custom-call | tf_op jit(solution)/shard_map/moments/pallas_call | solution.py:497
  (98 shorter events, 42.6 us)
Async XLA Ops:
  2.7 69.0 %all-to-all-start = ((bf16[64,3,48,128]{3,2,1,0:T(8,128)(2,1)}), bf16[64,3,48,128]{3,2,1,0:T(8,128)(2,1)S(1)}, u32[]{:S(2)}, u32[]{:S(2)}) async-start(bf16[64,3,48,128]{3,2,1,0:T(8,128)(2,1)} %pack_wide.1), calls=%async_computation | async-start | bytes 4718592 | tf_op jit(solution)/shard_map/all_to_all | solution.py:563
  17.1 36.7 %collective-permute-start.14 = (bf16[48,64,128]{2,1,0:T(8,128)(2,1)}, bf16[48,64,128]{2,1,0:T(8,128)(2,1)}, u32[]{:S(2)}, u32[]{:S(2)}) collective-permute-start(bf16[48,64,128]{2,1,0:T(8,128)(2,1)} %get-tuple-element.52.refs_8_.own_ref.rest_9_.base_ref), channel_id=1, source_target_pairs={{0,1},{1,2},{2,3},{3,0},{4,5},{5,6},{6,7},{7,4},{8,9},{9,10},{10,1... | collective-permute-start | bytes 2359304 | tf_op jit(solution)/shard_map/ppermute | solution.py:569
  18.5 35.4 %collective-permute-start.15 = (bf16[48,64,128]{2,1,0:T(8,128)(2,1)}, bf16[48,64,128]{2,1,0:T(8,128)(2,1)}, u32[]{:S(2)}, u32[]{:S(2)}) collective-permute-start(bf16[48,64,128]{2,1,0:T(8,128)(2,1)} %get-tuple-element.52.refs_8_.own_ref.rest_9_.base_ref), channel_id=1, source_target_pairs={{0,2},{1,3},{2,0},{3,1},{4,6},{5,7},{6,4},{7,5},{8,10},{9,11},{10,... | collective-permute-start | bytes 2359304 | tf_op jit(solution)/shard_map/ppermute | solution.py:569
  19.1 36.6 %collective-permute-start.16 = (bf16[48,64,128]{2,1,0:T(8,128)(2,1)}, bf16[48,64,128]{2,1,0:T(8,128)(2,1)}, u32[]{:S(2)}, u32[]{:S(2)}) collective-permute-start(bf16[48,64,128]{2,1,0:T(8,128)(2,1)} %get-tuple-element.52.refs_8_.own_ref.rest_9_.base_ref), channel_id=1, source_target_pairs={{0,3},{1,0},{2,1},{3,2},{4,7},{5,4},{6,5},{7,6},{8,11},{9,8},{10,9... | collective-permute-start | bytes 2359304 | tf_op jit(solution)/shard_map/ppermute | solution.py:569
  77.2 162.6 %all-to-all-start.1 = ((bf16[64,3,48,128]{3,2,1,0:T(8,128)(2,1)}), bf16[64,3,48,128]{3,2,1,0:T(8,128)(2,1)S(1)}, u32[]{:S(2)}, u32[]{:S(2)}) async-start(bf16[64,3,48,128]{3,2,1,0:T(8,128)(2,1)} %get-tuple-element.78), calls=%async_computation.1 | async-start | bytes 4718592 | tf_op jit(solution)/shard_map/all_to_all | solution.py:563
  82.9 11.2 %collective-permute-start.1 = (bf16[24,16,128]{2,1,0:T(8,128)(2,1)S(1)}, bf16[24,16,128]{2,1,0:T(8,128)(2,1)S(1)}, u32[]{:S(2)}, u32[]{:S(2)}) collective-permute-start(bf16[24,16,128]{2,1,0:T(8,128)(2,1)S(1)} %copy-done.18), channel_id=1, source_target_pairs={{0,8},{4,12},{8,16},{12,20},{16,24},{20,28},{24,0},{28,4},{32,40},... | collective-permute-start | bytes 294920 | tf_op jit(solution)/shard_map/ppermute | solution.py:516
  84.5 12.4 %collective-permute-start.2 = (bf16[24,16,128]{2,1,0:T(8,128)(2,1)S(1)}, bf16[24,16,128]{2,1,0:T(8,128)(2,1)S(1)}, u32[]{:S(2)}, u32[]{:S(2)}) collective-permute-start(bf16[24,16,128]{2,1,0:T(8,128)(2,1)S(1)} %copy-done.17), channel_id=1, source_target_pairs={{0,12},{4,8},{8,20},{12,16},{16,28},{20,24},{24,4},{28,0},{32,44},... | collective-permute-start | bytes 294920 | tf_op jit(solution)/shard_map/ppermute | solution.py:516
  85.7 17.3 %collective-permute-start.3 = (bf16[24,16,128]{2,1,0:T(8,128)(2,1)S(1)}, bf16[24,16,128]{2,1,0:T(8,128)(2,1)S(1)}, u32[]{:S(2)}, u32[]{:S(2)}) collective-permute-start(bf16[24,16,128]{2,1,0:T(8,128)(2,1)S(1)} %copy-done.16), channel_id=1, source_target_pairs={{0,16},{4,20},{8,24},{12,28},{16,0},{20,4},{24,8},{28,12},{32,48},... | collective-permute-start | bytes 294920 | tf_op jit(solution)/shard_map/ppermute | solution.py:516
  87.4 17.4 %collective-permute-start.4 = (bf16[24,16,128]{2,1,0:T(8,128)(2,1)S(1)}, bf16[24,16,128]{2,1,0:T(8,128)(2,1)S(1)}, u32[]{:S(2)}, u32[]{:S(2)}) collective-permute-start(bf16[24,16,128]{2,1,0:T(8,128)(2,1)S(1)} %copy-done.15), channel_id=1, source_target_pairs={{0,20},{4,16},{8,28},{12,24},{16,4},{20,0},{24,12},{28,8},{32,52},... | collective-permute-start | bytes 294920 | tf_op jit(solution)/shard_map/ppermute | solution.py:516
  89.0 15.8 %collective-permute-start.5 = (bf16[24,16,128]{2,1,0:T(8,128)(2,1)S(1)}, bf16[24,16,128]{2,1,0:T(8,128)(2,1)S(1)}, u32[]{:S(2)}, u32[]{:S(2)}) collective-permute-start(bf16[24,16,128]{2,1,0:T(8,128)(2,1)S(1)} %copy-done.14), channel_id=1, source_target_pairs={{0,24},{4,28},{8,0},{12,4},{16,8},{20,12},{24,16},{28,20},{32,56},... | collective-permute-start | bytes 294920 | tf_op jit(solution)/shard_map/ppermute | solution.py:516
  94.1 10.7 %collective-permute-start.6 = (bf16[24,16,128]{2,1,0:T(8,128)(2,1)S(1)}, bf16[24,16,128]{2,1,0:T(8,128)(2,1)S(1)}, u32[]{:S(2)}, u32[]{:S(2)}) collective-permute-start(bf16[24,16,128]{2,1,0:T(8,128)(2,1)S(1)} %copy-done.13), channel_id=1, source_target_pairs={{0,28},{4,24},{8,4},{12,0},{16,12},{20,8},{24,20},{28,16},{32,60},... | collective-permute-start | bytes 294920 | tf_op jit(solution)/shard_map/ppermute | solution.py:516
  106.8 37.6 %collective-permute-start.10 = (bf16[24,16,128]{2,1,0:T(8,128)(2,1)}, bf16[24,16,128]{2,1,0:T(8,128)(2,1)S(1)}, u32[]{:S(2)}, u32[]{:S(2)}) collective-permute-start(bf16[24,16,128]{2,1,0:T(8,128)(2,1)} %get-tuple-element.57), channel_id=1, source_target_pairs={{0,128},{4,132},{8,136},{12,140},{16,144},{20,148},{24,152},{28,15... | collective-permute-start | bytes 294920 | tf_op jit(solution)/shard_map/ppermute | solution.py:522
  115.0 31.5 %collective-permute-start.11 = (bf16[24,16,128]{2,1,0:T(8,128)(2,1)}, bf16[24,16,128]{2,1,0:T(8,128)(2,1)S(1)}, u32[]{:S(2)}, u32[]{:S(2)}) collective-permute-start(bf16[24,16,128]{2,1,0:T(8,128)(2,1)} %get-tuple-element.58), channel_id=1, source_target_pairs={{0,160},{4,164},{8,168},{12,172},{16,176},{20,180},{24,184},{28,18... | collective-permute-start | bytes 294920 | tf_op jit(solution)/shard_map/ppermute | solution.py:522
  115.0 36.7 %collective-permute-start.12 = (bf16[24,16,128]{2,1,0:T(8,128)(2,1)}, bf16[24,16,128]{2,1,0:T(8,128)(2,1)S(1)}, u32[]{:S(2)}, u32[]{:S(2)}) collective-permute-start(bf16[24,16,128]{2,1,0:T(8,128)(2,1)} %get-tuple-element.59), channel_id=1, source_target_pairs={{0,192},{4,196},{8,200},{12,204},{16,208},{20,212},{24,216},{28,22... | collective-permute-start | bytes 294920 | tf_op jit(solution)/shard_map/ppermute | solution.py:522
  118.1 34.5 %collective-permute-start.13 = (bf16[24,16,128]{2,1,0:T(8,128)(2,1)}, bf16[24,16,128]{2,1,0:T(8,128)(2,1)S(1)}, u32[]{:S(2)}, u32[]{:S(2)}) collective-permute-start(bf16[24,16,128]{2,1,0:T(8,128)(2,1)} %get-tuple-element.60), channel_id=1, source_target_pairs={{0,224},{4,228},{8,232},{12,236},{16,240},{20,244},{24,248},{28,25... | collective-permute-start | bytes 294920 | tf_op jit(solution)/shard_map/ppermute | solution.py:522
  119.6 33.0 %collective-permute-start.7 = (bf16[24,16,128]{2,1,0:T(8,128)(2,1)}, bf16[24,16,128]{2,1,0:T(8,128)(2,1)S(1)}, u32[]{:S(2)}, u32[]{:S(2)}) collective-permute-start(bf16[24,16,128]{2,1,0:T(8,128)(2,1)} %get-tuple-element.54), channel_id=1, source_target_pairs={{0,32},{4,36},{8,40},{12,44},{16,48},{20,52},{24,56},{28,60},{32,6... | collective-permute-start | bytes 294920 | tf_op jit(solution)/shard_map/ppermute | solution.py:522
  144.4 10.7 %collective-permute-start.8 = (bf16[24,16,128]{2,1,0:T(8,128)(2,1)}, bf16[24,16,128]{2,1,0:T(8,128)(2,1)S(1)}, u32[]{:S(2)}, u32[]{:S(2)}) collective-permute-start(bf16[24,16,128]{2,1,0:T(8,128)(2,1)} %get-tuple-element.55), channel_id=1, source_target_pairs={{0,64},{4,68},{8,72},{12,76},{16,80},{20,84},{24,88},{28,92},{32,9... | collective-permute-start | bytes 294920 | tf_op jit(solution)/shard_map/ppermute | solution.py:522
  146.5 9.0 %collective-permute-start.9 = (bf16[24,16,128]{2,1,0:T(8,128)(2,1)}, bf16[24,16,128]{2,1,0:T(8,128)(2,1)S(1)}, u32[]{:S(2)}, u32[]{:S(2)}) collective-permute-start(bf16[24,16,128]{2,1,0:T(8,128)(2,1)} %get-tuple-element.56), channel_id=1, source_target_pairs={{0,96},{4,100},{8,104},{12,108},{16,112},{20,116},{24,120},{28,124... | collective-permute-start | bytes 294920 | tf_op jit(solution)/shard_map/ppermute | solution.py:522
  162.7 9.6 %collective-permute-start.18 = (bf16[24,16,128]{2,1,0:T(8,128)(2,1)}, bf16[24,16,128]{2,1,0:T(8,128)(2,1)S(1)}, u32[]{:S(2)}, u32[]{:S(2)}) collective-permute-start(bf16[24,16,128]{2,1,0:T(8,128)(2,1)} %get-tuple-element.63), channel_id=1, source_target_pairs={{0,8},{4,12},{8,16},{12,20},{16,24},{20,28},{24,0},{28,4},{32,40},... | collective-permute-start | bytes 294920 | tf_op jit(solution)/shard_map/ppermute | solution.py:516
  167.8 9.9 %collective-permute-start.20 = (bf16[24,16,128]{2,1,0:T(8,128)(2,1)}, bf16[24,16,128]{2,1,0:T(8,128)(2,1)S(1)}, u32[]{:S(2)}, u32[]{:S(2)}) collective-permute-start(bf16[24,16,128]{2,1,0:T(8,128)(2,1)} %get-tuple-element.65), channel_id=1, source_target_pairs={{0,16},{4,20},{8,24},{12,28},{16,0},{20,4},{24,8},{28,12},{32,48},... | collective-permute-start | bytes 294920 | tf_op jit(solution)/shard_map/ppermute | solution.py:516
  169.7 9.0 %collective-permute-start.21 = (bf16[24,16,128]{2,1,0:T(8,128)(2,1)}, bf16[24,16,128]{2,1,0:T(8,128)(2,1)S(1)}, u32[]{:S(2)}, u32[]{:S(2)}) collective-permute-start(bf16[24,16,128]{2,1,0:T(8,128)(2,1)} %get-tuple-element.66), channel_id=1, source_target_pairs={{0,20},{4,16},{8,28},{12,24},{16,4},{20,0},{24,12},{28,8},{32,52},... | collective-permute-start | bytes 294920 | tf_op jit(solution)/shard_map/ppermute | solution.py:516
  171.1 56.3 %collective-permute-start.31 = (bf16[48,48,128]{2,1,0:T(8,128)(2,1)S(1)}, bf16[48,48,128]{2,1,0:T(8,128)(2,1)S(1)}, u32[]{:S(2)}, u32[]{:S(2)}) collective-permute-start(bf16[48,48,128]{2,1,0:T(8,128)(2,1)S(1)} %copy-done.3), channel_id=1, source_target_pairs={{0,1},{1,2},{2,3},{3,0},{4,5},{5,6},{6,7},{7,4},{8,9},{9,10},{10,1... | collective-permute-start | bytes 1769480 | tf_op jit(solution)/shard_map/ppermute | solution.py:569
  172.4 59.6 %collective-permute-start.32 = (bf16[48,48,128]{2,1,0:T(8,128)(2,1)S(1)}, bf16[48,48,128]{2,1,0:T(8,128)(2,1)S(1)}, u32[]{:S(2)}, u32[]{:S(2)}) collective-permute-start(bf16[48,48,128]{2,1,0:T(8,128)(2,1)S(1)} %copy-done.3), channel_id=1, source_target_pairs={{0,2},{1,3},{2,0},{3,1},{4,6},{5,7},{6,4},{7,5},{8,10},{9,11},{10,... | collective-permute-start | bytes 1769480 | tf_op jit(solution)/shard_map/ppermute | solution.py:569
  173.6 58.4 %collective-permute-start.33 = (bf16[48,48,128]{2,1,0:T(8,128)(2,1)S(1)}, bf16[48,48,128]{2,1,0:T(8,128)(2,1)S(1)}, u32[]{:S(2)}, u32[]{:S(2)}) collective-permute-start(bf16[48,48,128]{2,1,0:T(8,128)(2,1)S(1)} %copy-done.3), channel_id=1, source_target_pairs={{0,3},{1,0},{2,1},{3,2},{4,7},{5,4},{6,5},{7,6},{8,11},{9,8},{10,9... | collective-permute-start | bytes 1769480 | tf_op jit(solution)/shard_map/ppermute | solution.py:569
  178.7 25.4 %collective-permute-start.34 = (bf16[48,16,128]{2,1,0:T(8,128)(2,1)}, bf16[48,16,128]{2,1,0:T(8,128)(2,1)S(1)}, u32[]{:S(2)}, u32[]{:S(2)}) collective-permute-start(bf16[48,16,128]{2,1,0:T(8,128)(2,1)} %get-tuple-element.69.refs_8_.rest_4_), channel_id=1, source_target_pairs={{0,1},{1,2},{2,3},{3,0},{4,5},{5,6},{6,7},{7,4},{8,9},{9,10},{10,1... | collective-permute-start | bytes 589832 | tf_op jit(solution)/shard_map/ppermute | solution.py:569
  186.8 21.0 %collective-permute-start.35 = (bf16[48,16,128]{2,1,0:T(8,128)(2,1)}, bf16[48,16,128]{2,1,0:T(8,128)(2,1)S(1)}, u32[]{:S(2)}, u32[]{:S(2)}) collective-permute-start(bf16[48,16,128]{2,1,0:T(8,128)(2,1)} %get-tuple-element.69.refs_8_.rest_4_), channel_id=1, source_target_pairs={{0,2},{1,3},{2,0},{3,1},{4,6},{5,7},{6,4},{7,5},{8,10},{9,11},{10,... | collective-permute-start | bytes 589832 | tf_op jit(solution)/shard_map/ppermute | solution.py:569
  210.9 9.9 %collective-permute-start.25 = (bf16[24,16,128]{2,1,0:T(8,128)(2,1)}, bf16[24,16,128]{2,1,0:T(8,128)(2,1)S(1)}, u32[]{:S(2)}, u32[]{:S(2)}) collective-permute-start(bf16[24,16,128]{2,1,0:T(8,128)(2,1)} %get-tuple-element.72), channel_id=1, source_target_pairs={{0,64},{4,68},{8,72},{12,76},{16,80},{20,84},{24,88},{28,92},{32,9... | collective-permute-start | bytes 294920 | tf_op jit(solution)/shard_map/ppermute | solution.py:522
  214.0 29.4 %collective-permute-start.26 = (bf16[24,16,128]{2,1,0:T(8,128)(2,1)}, bf16[24,16,128]{2,1,0:T(8,128)(2,1)S(1)}, u32[]{:S(2)}, u32[]{:S(2)}) collective-permute-start(bf16[24,16,128]{2,1,0:T(8,128)(2,1)} %get-tuple-element.73), channel_id=1, source_target_pairs={{0,96},{4,100},{8,104},{12,108},{16,112},{20,116},{24,120},{28,124... | collective-permute-start | bytes 294920 | tf_op jit(solution)/shard_map/ppermute | solution.py:522
  220.8 22.6 %collective-permute-start.27 = (bf16[24,16,128]{2,1,0:T(8,128)(2,1)}, bf16[24,16,128]{2,1,0:T(8,128)(2,1)S(1)}, u32[]{:S(2)}, u32[]{:S(2)}) collective-permute-start(bf16[24,16,128]{2,1,0:T(8,128)(2,1)} %get-tuple-element.74), channel_id=1, source_target_pairs={{0,128},{4,132},{8,136},{12,140},{16,144},{20,148},{24,152},{28,15... | collective-permute-start | bytes 294920 | tf_op jit(solution)/shard_map/ppermute | solution.py:522
  227.4 16.0 %collective-permute-start.28 = (bf16[24,16,128]{2,1,0:T(8,128)(2,1)}, bf16[24,16,128]{2,1,0:T(8,128)(2,1)S(1)}, u32[]{:S(2)}, u32[]{:S(2)}) collective-permute-start(bf16[24,16,128]{2,1,0:T(8,128)(2,1)} %get-tuple-element.75), channel_id=1, source_target_pairs={{0,160},{4,164},{8,168},{12,172},{16,176},{20,180},{24,184},{28,18... | collective-permute-start | bytes 294920 | tf_op jit(solution)/shard_map/ppermute | solution.py:522
  232.0 11.5 %collective-permute-start.29 = (bf16[24,16,128]{2,1,0:T(8,128)(2,1)}, bf16[24,16,128]{2,1,0:T(8,128)(2,1)S(1)}, u32[]{:S(2)}, u32[]{:S(2)}) collective-permute-start(bf16[24,16,128]{2,1,0:T(8,128)(2,1)} %get-tuple-element.76), channel_id=1, source_target_pairs={{0,192},{4,196},{8,200},{12,204},{16,208},{20,212},{24,216},{28,22... | collective-permute-start | bytes 294920 | tf_op jit(solution)/shard_map/ppermute | solution.py:522
  232.0 11.5 %collective-permute-start.30 = (bf16[24,16,128]{2,1,0:T(8,128)(2,1)}, bf16[24,16,128]{2,1,0:T(8,128)(2,1)S(1)}, u32[]{:S(2)}, u32[]{:S(2)}) collective-permute-start(bf16[24,16,128]{2,1,0:T(8,128)(2,1)} %get-tuple-element.77), channel_id=1, source_target_pairs={{0,224},{4,228},{8,232},{12,236},{16,240},{20,244},{24,248},{28,25... | collective-permute-start | bytes 294920 | tf_op jit(solution)/shard_map/ppermute | solution.py:522
  (27 other events, 338.4 us)
